TPU v7x, 128 devices: a whole 4x4x4 slice. The times are simulated.
128 devices in a mesh: seq: 16 (over z, x), head: 8 (over y, core).
Axes of the slice: x: 4, y: 4, z: 4, core: 2. Of those that a mesh axis runs over, the one named last changes fastest.
Arguments:
- queries: bfloat16 [16384, 32, 128], P('seq', 'head'), may hold values from -6 to 6
- seg_keys: bfloat16 [16384, 32, 128], P('seq', 'head'), may hold values from -6 to 6
- seg_values: bfloat16 [16384, 32, 128], P('seq', 'head'), may hold values from -6 to 6
- mem_keys: bfloat16 [65536, 32, 128], P('seq', 'head'), may hold values from -6 to 6
- mem_values: bfloat16 [65536, 32, 128], P('seq', 'head'), may hold values from -6 to 6
- mem_blocks: int32 [128, 4], P(('seq', 'head')), may hold values from 0 to 511, as said below
- mem_count: int32 [128], P(('seq', 'head')), may hold values from 1 to 4, as said below
- grad_out: bfloat16 [16384, 32, 128], P('seq', 'head'), may hold values from -6 to 6
Outputs:
- attn_out: bfloat16 [16384, 32, 128], P('seq', 'head')
- grad_q: bfloat16 [16384, 32, 128], P('seq', 'head')
- grad_k: bfloat16 [16384, 32, 128], P('seq', 'head')
- grad_v: bfloat16 [16384, 32, 128], P('seq', 'head')
Inputs may be any that keep to these rules, and one draw needn't show every extreme that they name: `mem_blocks`: block n is held by owner n // 32. Among the 32 entries of the 8 query blocks of one seq shard (aligned blocks of 8 rows), at most 4 lie with one owner, and one owner has exactly 4 from every shard. Among the used entries (s < mem_count) of one seq shard at most 2 lie with one owner, and that same owner has exactly 2 used entries from every shard. `mem_count`: the counts of the 8 query blocks of one seq shard (aligned blocks of 8 rows) add up to 20, and in every such block of rows one count is 4.
All inputs are finite; a program needn't handle non-finite values.
Results may differ from a plain program's by a relative error of at most 0.012.
Values may be sent and summed in bfloat16 or wider, within the bound.
A program may use at most 192 MiB of HBM per device.

v0:
```python
import math

import jax
import jax.numpy as jnp
from jax import lax
from jax.sharding import PartitionSpec as P

WINDOW = 1024
BLOCK = 128
TOPK = 4


def passed_along(block, axis, distance):
    devices = range(lax.axis_size(axis))
    route = [(i - distance, i) for i in devices if i - distance in devices]
    return lax.ppermute(block, axis, route)


def fetch_memory(block_lists, block_counts, mem_keys, mem_values, owners, live_capacity):
    n_rows, top_count = block_lists.shape
    mem_local = mem_keys.shape[0] // BLOCK
    head_count = mem_keys.shape[1]
    head_dim = mem_keys.shape[2]
    flat_ids = block_lists.reshape(-1)
    owner_of = flat_ids // mem_local
    inside_id = flat_ids % mem_local
    one_hot = (owner_of[:, None] == jnp.arange(owners, dtype=jnp.int32)[None, :]).astype(jnp.int32)
    key_blocks = mem_keys.reshape(mem_local, BLOCK, head_count, head_dim)
    value_blocks = mem_values.reshape(mem_local, BLOCK, head_count, head_dim)
    live_flag = (jnp.arange(top_count, dtype=jnp.int32)[None, :] < block_counts[:, None]).reshape(
        -1
    )
    live_hot = one_hot * live_flag.astype(jnp.int32)[:, None]
    order_in = jnp.sum((jnp.cumsum(live_hot, 0) - 1) * live_hot, 1)
    slot_of = jnp.where(live_flag, owner_of * live_capacity + order_in, owners * live_capacity)
    send_table = (
        jnp.zeros((owners * live_capacity,), jnp.int32)
        .at[slot_of]
        .set(inside_id, mode="drop")
        .reshape(owners, live_capacity)
    )
    wanted = lax.all_to_all(send_table, "seq", split_axis=0, concat_axis=0, tiled=True)
    got_keys = lax.all_to_all(
        jnp.take(key_blocks, wanted, axis=0), "seq", split_axis=0, concat_axis=0, tiled=True
    )
    got_values = lax.all_to_all(
        jnp.take(value_blocks, wanted, axis=0), "seq", split_axis=0, concat_axis=0, tiled=True
    )
    read_slot = jnp.where(live_flag, slot_of, 0)
    got_keys = got_keys.reshape(owners * live_capacity, BLOCK, head_count, head_dim)[read_slot]
    got_values = got_values.reshape(owners * live_capacity, BLOCK, head_count, head_dim)[read_slot]
    got_keys = got_keys.reshape(n_rows, top_count * BLOCK, head_count, head_dim)
    got_values = got_values.reshape(n_rows, top_count * BLOCK, head_count, head_dim)
    return (jnp.moveaxis(got_keys, 2, 0), jnp.moveaxis(got_values, 2, 0))


def shards(queries, seg_keys, seg_values, mem_keys, mem_values, mem_blocks, mem_count, grad_out):
    local_tokens, head_count, head_dim = queries.shape
    owners = lax.axis_size("seq")
    seq_rank = lax.axis_index("seq")
    n_blocks = local_tokens // BLOCK
    n_tiles = local_tokens // WINDOW
    mem_span = TOPK * BLOCK
    live_total = n_blocks * (TOPK + 1) // 2
    live_capacity = max(2, 2 * live_total // owners)
    score_scale = 1.0 / math.sqrt(head_dim)
    block_lists, block_counts = (
        lax.all_gather(mem_blocks, "head", axis=0, tiled=True),
        lax.all_gather(mem_count, "head", axis=0, tiled=True),
    )
    prev_keys, prev_values = passed_along((seg_keys, seg_values), "seq", 1)
    keys_major = jnp.moveaxis(jnp.concatenate([prev_keys, seg_keys], 0), 1, 0)
    values_major = jnp.moveaxis(jnp.concatenate([prev_values, seg_values], 0), 1, 0)
    queries_major = jnp.moveaxis(queries, 1, 0)
    grads_major = jnp.moveaxis(grad_out, 1, 0)
    row_in = jnp.arange(WINDOW, dtype=jnp.int32)[:, None]
    col_in = jnp.arange(WINDOW, dtype=jnp.int32)[None, :]
    key_glob = (
        seq_rank * local_tokens
        + jnp.arange(n_tiles, dtype=jnp.int32)[:, None, None] * WINDOW
        + col_in[None]
        - WINDOW
    )
    lower_mask = (col_in > row_in)[None] & (key_glob >= 0)
    upper_mask = col_in <= row_in
    mem_slot = jnp.arange(mem_span, dtype=jnp.int32) // BLOCK
    far_mask = mem_slot[None, None, :] < block_counts[:, None, None]
    mem_k, mem_v = fetch_memory(
        block_lists, block_counts, mem_keys, mem_values, owners, live_capacity
    )

    def score_parts(query_rows, key_rows, mem_key_rows):
        query_tiles = query_rows.reshape(n_tiles, WINDOW, head_dim)
        key_tiles = key_rows.reshape(n_tiles + 1, WINDOW, head_dim)
        lower = (
            jnp.einsum(
                "twd,tjd->twj", query_tiles, key_tiles[:-1], preferred_element_type=jnp.float32
            )
            * score_scale
        )
        upper = (
            jnp.einsum(
                "twd,tjd->twj", query_tiles, key_tiles[1:], preferred_element_type=jnp.float32
            )
            * score_scale
        )
        far = (
            jnp.einsum(
                "nbd,nmd->nbm",
                query_rows.reshape(n_blocks, BLOCK, head_dim),
                mem_key_rows,
                preferred_element_type=jnp.float32,
            )
            * score_scale
        )
        lower = jnp.where(lower_mask, lower, -jnp.inf)
        upper = jnp.where(upper_mask[None], upper, -jnp.inf)
        far = jnp.where(far_mask, far, -jnp.inf)
        return (lower, upper, far)

    def probabilities(lower, upper, far, lse_tiles):
        lower_p = jnp.exp(lower - lse_tiles[:, :, None])
        upper_p = jnp.exp(upper - lse_tiles[:, :, None])
        far_p = jnp.exp(far - lse_tiles.reshape(n_blocks, BLOCK)[:, :, None])
        return (lower_p, upper_p, far_p)

    def mix(lower_w, upper_w, far_w, key_rows, mem_rows):
        key_tiles = key_rows.reshape(n_tiles + 1, WINDOW, head_dim)
        total = jnp.einsum(
            "twj,tjd->twd", lower_w, key_tiles[:-1], preferred_element_type=jnp.float32
        )
        total = total + jnp.einsum(
            "twj,tjd->twd", upper_w, key_tiles[1:], preferred_element_type=jnp.float32
        )
        far_total = jnp.einsum("nbm,nmd->nbd", far_w, mem_rows, preferred_element_type=jnp.float32)
        return total.reshape(local_tokens, head_dim) + far_total.reshape(local_tokens, head_dim)

    def forward_head(packed):
        query_rows, key_rows, value_rows, mem_key_rows, mem_value_rows = packed
        lower, upper, far = score_parts(query_rows, key_rows, mem_key_rows)
        row_top = jnp.maximum(
            jnp.maximum(jnp.max(lower, 2), jnp.max(upper, 2)),
            jnp.max(far, 2).reshape(n_tiles, WINDOW),
        )
        row_sum = jnp.sum(jnp.exp(lower - row_top[:, :, None]), 2) + jnp.sum(
            jnp.exp(upper - row_top[:, :, None]), 2
        )
        row_sum = row_sum + jnp.sum(
            jnp.exp(far - row_top.reshape(n_blocks, BLOCK)[:, :, None]), 2
        ).reshape(n_tiles, WINDOW)
        lse_tiles = row_top + jnp.log(row_sum)
        lower_p, upper_p, far_p = probabilities(lower, upper, far, lse_tiles)
        attn_rows = mix(
            lower_p.astype(jnp.bfloat16),
            upper_p.astype(jnp.bfloat16),
            far_p.astype(jnp.bfloat16),
            value_rows,
            mem_value_rows,
        ).astype(jnp.bfloat16)
        return (attn_rows, lse_tiles.reshape(local_tokens))

    attn_heads, lse_heads = lax.map(
        forward_head, (queries_major, keys_major, values_major, mem_k, mem_v)
    )
    back_k, back_v = (mem_k, mem_v)

    def backward_head(packed):
        (
            query_rows,
            grad_rows,
            key_rows,
            value_rows,
            mem_key_rows,
            mem_value_rows,
            attn_rows,
            lse_rows,
        ) = packed
        lower, upper, far = score_parts(query_rows, key_rows, mem_key_rows)
        lse_tiles = lse_rows.reshape(n_tiles, WINDOW)
        lower_p, upper_p, far_p = probabilities(lower, upper, far, lse_tiles)
        delta_rows = jnp.sum(grad_rows.astype(jnp.float32) * attn_rows.astype(jnp.float32), 1)
        delta_tiles = delta_rows.reshape(n_tiles, WINDOW)
        grad_tiles = grad_rows.reshape(n_tiles, WINDOW, head_dim)
        query_tiles = query_rows.reshape(n_tiles, WINDOW, head_dim)
        value_tiles = value_rows.reshape(n_tiles + 1, WINDOW, head_dim)
        grad_blocks = grad_rows.reshape(n_blocks, BLOCK, head_dim)
        lower_dp = jnp.einsum(
            "twd,tjd->twj", grad_tiles, value_tiles[:-1], preferred_element_type=jnp.float32
        )
        upper_dp = jnp.einsum(
            "twd,tjd->twj", grad_tiles, value_tiles[1:], preferred_element_type=jnp.float32
        )
        far_dp = jnp.einsum(
            "nbd,nmd->nbm", grad_blocks, mem_value_rows, preferred_element_type=jnp.float32
        )
        lower_ds = (lower_p * (lower_dp - delta_tiles[:, :, None])).astype(jnp.bfloat16)
        upper_ds = (upper_p * (upper_dp - delta_tiles[:, :, None])).astype(jnp.bfloat16)
        far_ds = (far_p * (far_dp - delta_rows.reshape(n_blocks, BLOCK)[:, :, None])).astype(
            jnp.bfloat16
        )
        grad_query = (score_scale * mix(lower_ds, upper_ds, far_ds, key_rows, mem_key_rows)).astype(
            jnp.bfloat16
        )
        zero_tile = jnp.zeros((1, WINDOW, head_dim), jnp.float32)
        lower_kg = jnp.einsum(
            "twj,twd->tjd", lower_ds, query_tiles, preferred_element_type=jnp.float32
        )
        upper_kg = jnp.einsum(
            "twj,twd->tjd", upper_ds, query_tiles, preferred_element_type=jnp.float32
        )
        key_grad = score_scale * (
            jnp.concatenate([lower_kg, zero_tile], 0) + jnp.concatenate([zero_tile, upper_kg], 0)
        )
        lower_vg = jnp.einsum(
            "twj,twd->tjd",
            lower_p.astype(jnp.bfloat16),
            grad_tiles,
            preferred_element_type=jnp.float32,
        )
        upper_vg = jnp.einsum(
            "twj,twd->tjd",
            upper_p.astype(jnp.bfloat16),
            grad_tiles,
            preferred_element_type=jnp.float32,
        )
        value_grad = jnp.concatenate([lower_vg, zero_tile], 0) + jnp.concatenate(
            [zero_tile, upper_vg], 0
        )
        ext_rows = (n_tiles + 1) * WINDOW
        return (
            grad_query,
            key_grad.reshape(ext_rows, head_dim),
            value_grad.reshape(ext_rows, head_dim),
            delta_rows,
        )

    gradq_heads, key_ext, value_ext, delta_heads = lax.map(
        backward_head,
        (
            queries_major,
            grads_major,
            keys_major,
            values_major,
            back_k,
            back_v,
            attn_heads,
            lse_heads,
        ),
    )
    own_keys = key_ext[:, WINDOW:]
    own_values = value_ext[:, WINDOW:]
    back_keys, back_values = passed_along((key_ext[:, :WINDOW], value_ext[:, :WINDOW]), "seq", -1)
    own_keys = own_keys + back_keys
    own_values = own_values + back_values
    attn_out = jnp.moveaxis(attn_heads, 0, 1)
    grad_q = jnp.moveaxis(gradq_heads, 0, 1)
    grad_k = jnp.moveaxis(own_keys.astype(jnp.bfloat16), 0, 1)
    grad_v = jnp.moveaxis(own_values.astype(jnp.bfloat16), 0, 1)
    return (attn_out, grad_q, grad_k, grad_v)


def solution(mesh):
    return jax.shard_map(
        shards,
        mesh=mesh,
        in_specs=(
            P("seq", "head", None),
            P("seq", "head", None),
            P("seq", "head", None),
            P("seq", "head", None),
            P("seq", "head", None),
            P(("seq", "head"), None),
            P(("seq", "head")),
            P("seq", "head", None),
        ),
        out_specs=(
            P("seq", "head", None),
            P("seq", "head", None),
            P("seq", "head", None),
            P("seq", "head", None),
        ),
        check_vma=False,
    )
```

profile of v0, /device:TPU:6, one launch (start us, length us, event | category | flops | bytes accessed | tf_op | source)
XLA Modules:
  0.0 730.4 jit_solution(18352272048460690468)
XLA Ops:
  3.3 9.5 %all-reduce.4 = s32[8]{0:T(128)S(1)} all-reduce(s32[8]{0:T(128)S(1)} %dynamic-update-slice), channel_id=1, replica_groups=mesh['seq'=16,'head'=8] {'head'}, use_global_device_ids=true, to_apply=%add.4 | all-reduce | flops 8 | bytes 64
  12.8 8.5 %all-gather = s32[8,1,4]{2,1,0:T(1,128)S(1)} all-gather(s32[1,1,4]{2,1,0:T(1,128)} %bitcast.379), channel_id=1, replica_groups=mesh['seq'=16,'head'=8] {'head'}, dimensions={0}, use_global_device_ids=true | all-gather | bytes 144 | tf_op jit(solution)/shard_map/all_gather | solution.py:68
  24.0 13.6 %all_to_all.22 = s32[16,1,2]{2,1,0:T(1,128)S(1)} all-to-all(s32[16,1,2]{2,1,0:T(1,128)S(1)} %bitcast.378), channel_id=1, replica_groups=mesh['seq'=16,'head'=8] {'seq'}, dimensions={0} | all-to-all | bytes 256 | tf_op jit(solution)/shard_map/all_to_all | solution.py:42
  38.0 8.0 %gather_fusion.3 = bf16[32,128,4,128]{3,2,1,0:T(4,128)(2,1)} fusion(bf16[32,128,4,128]{3,2,1,0:T(4,128)(2,1)} %bitcast.363, s32[1024]{0:T(1024)S(1)} %pad_clamp_fusion.1), kind=kCustom, calls=%fused_computation.1.clone | custom fusion | bytes 8388736 | tf_op jit(solution)/shard_map/jit(_take)/gather | solution.py:47
  46.0 5.3 copy.82
  51.3 8.0 %gather_fusion.2 = bf16[32,128,4,128]{3,2,1,0:T(4,128)(2,1)} fusion(bf16[32,128,4,128]{3,2,1,0:T(4,128)(2,1)} %bitcast.364, s32[1024]{0:T(1024)S(1)} %pad_clamp_fusion.1), kind=kCustom, calls=%fused_computation.clone | custom fusion | bytes 8388736 | tf_op jit(solution)/shard_map/jit(_take)/gather | solution.py:44
  59.2 3.5 copy.76
  65.1 52.8 %all_to_all.23 = bf16[16,2,128,4,128]{4,2,3,1,0:T(8,128)(2,1)} all-to-all(bf16[16,2,128,4,128]{4,2,3,1,0:T(8,128)(2,1)S(1)} %get-tuple-element.281), channel_id=1, replica_groups=mesh['seq'=16,'head'=8] {'seq'}, dimensions={0} | all-to-all | bytes 8388608 | tf_op jit(solution)/shard_map/all_to_all | solution.py:46
  117.9 7.4 %all-to-all-start.1 = ((bf16[16,2,128,4,128]{4,2,3,1,0:T(8,128)(2,1)}), bf16[16,2,128,4,128]{4,2,3,1,0:T(8,128)(2,1)}, u32[]{:S(2)}, u32[]{:S(2)}) async-start(bf16[16,2,128,4,128]{4,2,3,1,0:T(8,128)(2,1)} %get-tuple-element.282), calls=%async_computation.1 | async-start | bytes 8388608 | tf_op jit(solution)/shard_map/all_to_all | solution.py:43
  125.5 3.4 collective-permute-start.1
  129.1 3.6 collective-permute-start
  132.7 3.1 copy_bitcast_fusion.1
  135.8 71.2 %collective-permute-done.1 = bf16[1024,4,128]{2,0,1:T(8,128)(2,1)} collective-permute-done((bf16[1024,4,128]{2,0,1:T(8,128)(2,1)S(1)}, bf16[1024,4,128]{2,0,1:T(8,128)(2,1)}, u32[]{:S(2)}, u32[]{:S(2)}) %collective-permute-start.1) | collective-permute-done | bytes 1048608 | tf_op jit(solution)/shard_map/ppermute | solution.py:16
  209.7 16.8 %collective-permute-done = bf16[1024,4,128]{2,0,1:T(8,128)(2,1)S(1)} collective-permute-done((bf16[1024,4,128]{2,0,1:T(8,128)(2,1)S(1)}, bf16[1024,4,128]{2,0,1:T(8,128)(2,1)S(1)}, u32[]{:S(2)}, u32[]{:S(2)}) %collective-permute-start) | collective-permute-done | bytes 1048608 | tf_op jit(solution)/shard_map/ppermute | solution.py:16
  228.0 5.2 gather_fusion.1
  233.2 4.7 copy.83
  237.9 5.2 gather_fusion
  243.1 4.7 copy.77
  249.0 67.5 %while.28 = (s32[]{:T(128)}, bf16[4,1024,128]{2,1,0:T(8,128)(2,1)}, f32[4,1024]{1,0:T(4,128)S(1)}, bf16[4,1024,128]{2,1,0:T(8,128)(2,1)}, bf16[4,2048,128]{2,1,0...) while((s32[]{:T(128)}, bf16[4,1024,128]{2,1,0:T(8,128)(2,1)}, ...), condition=%wide.region_10.12_spmd.clone, body=%wide.region_3.11_spmd.clone.sunk | while | flops 1378756608 | bytes 38441680 | solution.py:162
  256.0 3.3 exponential_reduce_fusion.6
  262.9 2.9 fusion.177
  272.9 3.3 exponential_reduce_fusion.6
  279.8 2.9 fusion.177
  289.7 3.3 exponential_reduce_fusion.6
  296.6 2.9 fusion.177
  306.6 3.3 exponential_reduce_fusion.6
  313.5 2.9 fusion.177
  317.6 315.7 %while.29 = (s32[]{:T(128)}, bf16[4,1024,128]{2,1,0:T(8,128)(2,1)}, f32[4,2048,128]{2,0,1:T(4,128)}, f32[4,2048,128]{2,0,1:T(4,128)}, bf16[4,1024,128]{2,1,0:T(8...) while((s32[]{:T(128)}, bf16[4,1024,128]{2,1,0:T(8,128)(2,1)}, ...), condition=%wide.region_13.15_spmd.clone, body=%wide.region_11.14_spmd.clone.sunk | while | flops 3119254528 | bytes 63499020 | solution.py:237
  326.8 2.9 multiply_convert_fusion.6
  333.2 3.2 multiply_convert_fusion.5
  341.4 27.6 %dynamic_update_slice.33 = f32[4,2048,128]{2,0,1:T(4,128)} dynamic-update-slice(f32[4,2048,128]{2,0,1:T(4,128)} %get-tuple-element.537, f32[1,2048,128]{2,0,1:T(1,128)S(1)} %bitcast.353, s32[]{:T(128)S(6)} %copy.120, s32[]{:T(128)} %constant.118.clone.1..sunk.1, s32[]{:T(128)} %constant.118.clone.1..sunk.1) | dynamic-update-slice | bytes 2097156 | tf_op jit(solution)/shard_map/while/body/jit(dynamic_update_index_in_dim)/dynamic_update_slice | solution.py:237
  369.0 27.5 %dynamic_update_slice.34 = f32[4,2048,128]{2,0,1:T(4,128)} dynamic-update-slice(f32[4,2048,128]{2,0,1:T(4,128)} %get-tuple-element.538, f32[1,2048,128]{2,0,1:T(1,128)S(1)} %bitcast.352, s32[]{:T(128)S(6)} %copy.120, s32[]{:T(128)} %constant.118.clone.1..sunk.1, s32[]{:T(128)} %constant.118.clone.1..sunk.1) | dynamic-update-slice | bytes 2097156 | tf_op jit(solution)/shard_map/while/body/jit(dynamic_update_index_in_dim)/dynamic_update_slice | solution.py:237
  405.7 2.9 multiply_convert_fusion.6
  412.1 3.2 multiply_convert_fusion.5
  420.3 27.6 %dynamic_update_slice.33 = f32[4,2048,128]{2,0,1:T(4,128)} dynamic-update-slice(f32[4,2048,128]{2,0,1:T(4,128)} %get-tuple-element.537, f32[1,2048,128]{2,0,1:T(1,128)S(1)} %bitcast.353, s32[]{:T(128)S(6)} %copy.120, s32[]{:T(128)} %constant.118.clone.1..sunk.1, s32[]{:T(128)} %constant.118.clone.1..sunk.1) | dynamic-update-slice | bytes 2097156 | tf_op jit(solution)/shard_map/while/body/jit(dynamic_update_index_in_dim)/dynamic_update_slice | solution.py:237
  447.9 27.5 %dynamic_update_slice.34 = f32[4,2048,128]{2,0,1:T(4,128)} dynamic-update-slice(f32[4,2048,128]{2,0,1:T(4,128)} %get-tuple-element.538, f32[1,2048,128]{2,0,1:T(1,128)S(1)} %bitcast.352, s32[]{:T(128)S(6)} %copy.120, s32[]{:T(128)} %constant.118.clone.1..sunk.1, s32[]{:T(128)} %constant.118.clone.1..sunk.1) | dynamic-update-slice | bytes 2097156 | tf_op jit(solution)/shard_map/while/body/jit(dynamic_update_index_in_dim)/dynamic_update_slice | solution.py:237
  484.6 2.9 multiply_convert_fusion.6
  491.0 3.2 multiply_convert_fusion.5
  499.2 27.6 %dynamic_update_slice.33 = f32[4,2048,128]{2,0,1:T(4,128)} dynamic-update-slice(f32[4,2048,128]{2,0,1:T(4,128)} %get-tuple-element.537, f32[1,2048,128]{2,0,1:T(1,128)S(1)} %bitcast.353, s32[]{:T(128)S(6)} %copy.120, s32[]{:T(128)} %constant.118.clone.1..sunk.1, s32[]{:T(128)} %constant.118.clone.1..sunk.1) | dynamic-update-slice | bytes 2097156 | tf_op jit(solution)/shard_map/while/body/jit(dynamic_update_index_in_dim)/dynamic_update_slice | solution.py:237
  526.8 27.5 %dynamic_update_slice.34 = f32[4,2048,128]{2,0,1:T(4,128)} dynamic-update-slice(f32[4,2048,128]{2,0,1:T(4,128)} %get-tuple-element.538, f32[1,2048,128]{2,0,1:T(1,128)S(1)} %bitcast.352, s32[]{:T(128)S(6)} %copy.120, s32[]{:T(128)} %constant.118.clone.1..sunk.1, s32[]{:T(128)} %constant.118.clone.1..sunk.1) | dynamic-update-slice | bytes 2097156 | tf_op jit(solution)/shard_map/while/body/jit(dynamic_update_index_in_dim)/dynamic_update_slice | solution.py:237
  563.5 2.9 multiply_convert_fusion.6
  569.9 3.2 multiply_convert_fusion.5
  578.2 27.6 %dynamic_update_slice.33 = f32[4,2048,128]{2,0,1:T(4,128)} dynamic-update-slice(f32[4,2048,128]{2,0,1:T(4,128)} %get-tuple-element.537, f32[1,2048,128]{2,0,1:T(1,128)S(1)} %bitcast.353, s32[]{:T(128)S(6)} %copy.120, s32[]{:T(128)} %constant.118.clone.1..sunk.1, s32[]{:T(128)} %constant.118.clone.1..sunk.1) | dynamic-update-slice | bytes 2097156 | tf_op jit(solution)/shard_map/while/body/jit(dynamic_update_index_in_dim)/dynamic_update_slice | solution.py:237
  605.7 27.5 %dynamic_update_slice.34 = f32[4,2048,128]{2,0,1:T(4,128)} dynamic-update-slice(f32[4,2048,128]{2,0,1:T(4,128)} %get-tuple-element.538, f32[1,2048,128]{2,0,1:T(1,128)S(1)} %bitcast.352, s32[]{:T(128)S(6)} %copy.120, s32[]{:T(128)} %constant.118.clone.1..sunk.1, s32[]{:T(128)} %constant.118.clone.1..sunk.1) | dynamic-update-slice | bytes 2097156 | tf_op jit(solution)/shard_map/while/body/jit(dynamic_update_index_in_dim)/dynamic_update_slice | solution.py:237
  639.7 3.0 copy.100
  642.7 3.0 copy.99
  645.7 42.0 %collective-permute-done.2 = f32[4,1024,128]{2,0,1:T(4,128)S(1)} collective-permute-done((f32[4,1024,128]{2,0,1:T(4,128)S(1)}, f32[4,1024,128]{2,0,1:T(4,128)S(1)}, u32[]{:S(2)}, u32[]{:S(2)}) %collective-permute-start.2) | collective-permute-done | bytes 2097184 | tf_op jit(solution)/shard_map/ppermute | solution.py:16
  689.2 39.7 %collective-permute-done.3 = f32[4,1024,128]{2,0,1:T(4,128)S(1)} collective-permute-done((f32[4,1024,128]{2,0,1:T(4,128)S(1)}, f32[4,1024,128]{2,0,1:T(4,128)S(1)}, u32[]{:S(2)}, u32[]{:S(2)}) %collective-permute-start.3) | collective-permute-done | bytes 2097184 | tf_op jit(solution)/shard_map/ppermute | solution.py:16
  (175 shorter events, 136.5 us)
Async XLA Ops:
  59.2 3.5 copy-start
  117.9 7.5 %copy-start.3 = (bf16[1024,4,128]{2,1,0:T(4,128)(2,1)S(1)}, bf16[1024,4,128]{2,1,0:T(4,128)(2,1)}, u32[]{:S(2)}) copy-start(bf16[1024,4,128]{2,1,0:T(4,128)(2,1)} %param.16) | copy-start | bytes 3145732
  117.9 11.0 %copy-start.4 = (bf16[1024,4,128]{2,1,0:T(4,128)(2,1)S(1)}, bf16[1024,4,128]{2,1,0:T(4,128)(2,1)}, u32[]{:S(2)}) copy-start(bf16[1024,4,128]{2,1,0:T(4,128)(2,1)} %param.15) | copy-start | bytes 3145732
  117.9 120.0 %all-to-all-start.1 = ((bf16[16,2,128,4,128]{4,2,3,1,0:T(8,128)(2,1)}), bf16[16,2,128,4,128]{4,2,3,1,0:T(8,128)(2,1)}, u32[]{:S(2)}, u32[]{:S(2)}) async-start(bf16[16,2,128,4,128]{4,2,3,1,0:T(8,128)(2,1)} %get-tuple-element.282), calls=%async_computation.1 | async-start | bytes 8388608 | tf_op jit(solution)/shard_map/all_to_all | solution.py:43
  125.5 81.5 %collective-permute-start.1 = (bf16[1024,4,128]{2,0,1:T(8,128)(2,1)S(1)}, bf16[1024,4,128]{2,0,1:T(8,128)(2,1)}, u32[]{:S(2)}, u32[]{:S(2)}) collective-permute-start(bf16[1024,4,128]{2,0,1:T(8,128)(2,1)S(1)} %copy.78), channel_id=1, source_target_pairs={{0,8},{8,16},{16,24},{24,32},{32,40},{40,48},{48,56},{56,64},{64,7... | collective-permute-start | bytes 3145736 | tf_op jit(solution)/shard_map/ppermute | solution.py:16
  129.1 97.5 %collective-permute-start = (bf16[1024,4,128]{2,0,1:T(8,128)(2,1)S(1)}, bf16[1024,4,128]{2,0,1:T(8,128)(2,1)S(1)}, u32[]{:S(2)}, u32[]{:S(2)}) collective-permute-start(bf16[1024,4,128]{2,0,1:T(8,128)(2,1)S(1)} %copy.70), channel_id=1, source_target_pairs={{0,8},{8,16},{16,24},{24,32},{32,40},{40,48},{48,56},{56,64},{64,7... | collective-permute-start | bytes 3145736 | tf_op jit(solution)/shard_map/ppermute | solution.py:16
  633.3 3.8 copy-start.1
  635.1 52.6 %collective-permute-start.2 = (f32[4,1024,128]{2,0,1:T(4,128)S(1)}, f32[4,1024,128]{2,0,1:T(4,128)S(1)}, u32[]{:S(2)}, u32[]{:S(2)}) collective-permute-start(f32[4,1024,128]{2,0,1:T(4,128)S(1)} %slice.47), channel_id=1, source_target_pairs={{8,0},{16,8},{24,16},{32,24},{40,32},{48,40},{56,48},{64,56},{72,6... | collective-permute-start | bytes 6291464 | tf_op jit(solution)/shard_map/ppermute | solution.py:16
  637.1 50.6 %copy-start.2 = (f32[4,2048,128]{2,0,1:T(4,128)S(1)}, f32[4,2048,128]{2,0,1:T(4,128)}, u32[]{:S(2)}) copy-start(f32[4,2048,128]{2,0,1:T(4,128)} %get-tuple-element.145) | copy-start | bytes 12582916
  637.2 91.7 %collective-permute-start.3 = (f32[4,1024,128]{2,0,1:T(4,128)S(1)}, f32[4,1024,128]{2,0,1:T(4,128)S(1)}, u32[]{:S(2)}, u32[]{:S(2)}) collective-permute-start(f32[4,1024,128]{2,0,1:T(4,128)S(1)} %slice.49), channel_id=1, source_target_pairs={{8,0},{16,8},{24,16},{32,24},{40,32},{48,40},{56,48},{64,56},{72,6... | collective-permute-start | bytes 6291464 | tf_op jit(solution)/shard_map/ppermute | solution.py:16
where the time goes:
time: 739 us; the launch traced here: 730 us
  local copies, waits for them, and re-layouts  291 us (39%)
  waiting for transfers between devices  170 us (23%)
  matrix products  132 us (18%)
  blocking collectives  84.4 us (11%)
  other arithmetic  33.1 us (4%)
  starting transfers between devices  18.7 us (3%)
    dynamic_update_slice x8, local copies, waits for them, and re-layouts, shards(): lax.map(backward_head, (queries_major, grads_major, keys_major, values_ma...  220 us
    ppermute x4, waiting for transfers between devices, passed_along(): return lax.ppermute(block, axis, route)  170 us
    all_to_all x1, blocking collectives, fetch_memory(): lax.all_to_all(jnp.take(value_blocks, wanted, axis=0), 'seq', split_axis=...  52.8 us
    dot_general x8, matrix products, mix(): jnp.einsum('twj,tjd->twd', lower_w, key_tiles[:-1], preferred_element_typ...  18.2 us
    dot_general x8, matrix products, mix(): jnp.einsum('nbm,nmd->nbd', far_w, mem_rows, preferred_element_type=jnp.fl...  17.2 us
    dot_general x8, matrix products, mix(): jnp.einsum('twj,tjd->twd', upper_w, key_tiles[1:], preferred_element_type...  16.6 us
  transfers between devices with their start and end apart: 5, of which 4 were waited for; matrix products, arithmetic and copies ran while one was open for 3% of the time, Pallas kernels for 0%

commit v1 on v0

v1 whole, which is shorter than its diff:
```python
import functools
import math

import jax
import jax.numpy as jnp
from jax import lax
from jax.experimental import pallas as pl
from jax.experimental.pallas import tpu as pltpu
from jax.sharding import PartitionSpec as P

WINDOW = 1024
BLOCK = 128
TOPK = 4
LIVE = 2
GROUP = 1
TILE = 256
VMEM = 58 * 1024 * 1024
NEG = -1e30
F32 = jnp.float32
BF16 = jnp.bfloat16
NT = (((1,), (1,)), ((), ()))
TN = (((0,), (0,)), ((), ()))


def rows_to_heads(rows, heads):
    out = lax.broadcasted_iota(jnp.int32, (rows, rows), 0)
    src = lax.broadcasted_iota(jnp.int32, (rows, rows), 1)
    per = rows // heads
    return (src == heads * (out % per) + out // per).astype(BF16)


def heads_to_rows(rows, heads):
    out = lax.broadcasted_iota(jnp.int32, (rows, rows), 0)
    src = lax.broadcasted_iota(jnp.int32, (rows, rows), 1)
    per = rows // heads
    return (src == per * (out % heads) + out // heads).astype(BF16)


def dot(a, b, dims=None):
    if dims is None:
        return jnp.dot(a, b, preferred_element_type=F32)
    return lax.dot_general(a, b, dims, preferred_element_type=F32)


def split_heads_body(heads, group, q_ref, d_ref, k_ref, v_ref, qo_ref, do_ref, *kv_refs):
    perm = rows_to_heads(256, heads)
    per = 256 // heads
    for part in range(q_ref.shape[0] // 256):
        src = pl.ds(part * 256, 256)
        dst = pl.ds(part * per, per)
        qd = dot(perm, jnp.concatenate([q_ref[src, :], d_ref[src, :]], 1)).astype(BF16)
        kv = dot(perm, jnp.concatenate([k_ref[src, :], v_ref[src, :]], 1)).astype(BF16)
        for h in range(heads):
            rows = slice(h * per, (h + 1) * per)
            qo_ref[h, dst, :] = qd[rows, :128]
            do_ref[h, dst, :] = qd[rows, 128:]
            kv_refs[h // group][0, h % group, dst, :] = kv[rows, :128]
            kv_refs[h // group][1, h % group, dst, :] = kv[rows, 128:]


def split_heads(q, d, k, v, heads, group):
    rows = q.shape[0]
    tokens = rows // heads
    steps = 4
    n_groups = heads // group
    in_spec = pl.BlockSpec((rows // steps, 128), lambda i: (i, 0))
    hm = pl.BlockSpec((heads, tokens // steps, 128), lambda i: (0, i, 0))
    kv = pl.BlockSpec((2, group, tokens // steps, 128), lambda i: (0, 0, i, 0))
    return pl.pallas_call(
        functools.partial(split_heads_body, heads, group),
        grid=(steps,),
        in_specs=[in_spec] * 4,
        out_specs=[hm, hm] + [kv] * n_groups,
        out_shape=[jax.ShapeDtypeStruct((heads, tokens, 128), BF16)] * 2
        + [jax.ShapeDtypeStruct((2, group, tokens, 128), BF16)] * n_groups,
        cost_estimate=pl.CostEstimate(
            flops=4 * 2 * rows * 256 * 128, bytes_accessed=16 * rows * 128, transcendentals=0
        ),
        compiler_params=pltpu.CompilerParams(vmem_limit_bytes=VMEM),
        name="split_heads",
    )(q, d, k, v)


def pick_body(heads, group, per_step, idx_ref, *refs):
    ins, outs = refs[: 2 * per_step], refs[2 * per_step :]
    perm = rows_to_heads(256, heads)
    per = 256 // heads
    for j in range(per_step):
        k_ref, v_ref = ins[2 * j], ins[2 * j + 1]
        for part in range(BLOCK * heads // 256):
            src = pl.ds(part * 256, 256)
            dst = pl.ds(part * per, per)
            kv = dot(perm, jnp.concatenate([k_ref[0, src, :], v_ref[0, src, :]], 1)).astype(BF16)
            for h in range(heads):
                rows = slice(h * per, (h + 1) * per)
                outs[h // group][j, 0, h % group, dst, :] = kv[rows, :128]
                outs[h // group][j, 1, h % group, dst, :] = kv[rows, 128:]


def pick_blocks(index, mem_k, mem_v, heads, group):
    slots = index.shape[0]
    per_step = 4
    n_groups = heads // group

    def at(j):
        return pl.BlockSpec(
            (1, BLOCK * heads, 128), lambda i, idx, j=j: (idx[i * per_step + j], 0, 0)
        )

    out = pl.BlockSpec((per_step, 2, group, BLOCK, 128), lambda i, idx: (i, 0, 0, 0, 0))
    ins = []
    for _ in range(per_step):
        ins += [mem_k, mem_v]
    return pl.pallas_call(
        functools.partial(pick_body, heads, group, per_step),
        grid_spec=pltpu.PrefetchScalarGridSpec(
            num_scalar_prefetch=1,
            grid=(slots // per_step,),
            in_specs=[at(j // 2) for j in range(2 * per_step)],
            out_specs=[out] * n_groups,
        ),
        out_shape=[jax.ShapeDtypeStruct((slots, 2, group, BLOCK, 128), BF16)] * n_groups,
        cost_estimate=pl.CostEstimate(
            flops=slots * 4 * BLOCK * heads * 256 * 128,
            bytes_accessed=slots * 8 * BLOCK * heads * 128,
            transcendentals=0,
        ),
        compiler_params=pltpu.CompilerParams(vmem_limit_bytes=VMEM),
        name="pick_blocks",
    )(index, *ins)


def attend_body(
    slot_ref, count_ref, rank_ref, q_ref, g_ref, own_ref, halo_ref, mem_ref,
    o_ref, dq_ref, back_ref, keep_ref,
    kx, vx, km, vm, s_ref, dp_ref, p_ref, ds_ref, ka, va,
):
    t = pl.program_id(1)
    span = WINDOW + TILE
    mem_span = TOPK * BLOCK
    total = span + mem_span
    halves = TILE // BLOCK
    scale = 1.0 / math.sqrt(128.0)
    to_two = scale * math.log2(math.e)

    @pl.when(t == 0)
    def _():
        kx[:WINDOW, :] = halo_ref[0, 0]
        kx[WINDOW:, :] = own_ref[0, 0]
        vx[:WINDOW, :] = halo_ref[1, 0]
        vx[WINDOW:, :] = own_ref[1, 0]
        ka[...] = jnp.zeros_like(ka)
        va[...] = jnp.zeros_like(va)

    start = pl.multiple_of(t * TILE, TILE)
    win = pl.ds(start, span)
    q = q_ref[0, pl.ds(start, TILE), :]
    g = g_ref[0, pl.ds(start, TILE), :]

    for half in range(halves):
        for e in range(TOPK):
            slot = slot_ref[(t * halves + half) * TOPK + e]
            km[half, e * BLOCK : (e + 1) * BLOCK, :] = mem_ref[slot, 0, 0]
            vm[half, e * BLOCK : (e + 1) * BLOCK, :] = mem_ref[slot, 1, 0]

    s_ref[:span, :] = dot(kx[win, :], q, NT)
    dp_ref[:span, :] = dot(vx[win, :], g, NT)
    for half in range(halves):
        cols = slice(half * BLOCK, (half + 1) * BLOCK)
        s_ref[span:, cols] = dot(km[half], q[cols], NT)
        dp_ref[span:, cols] = dot(vm[half], g[cols], NT)

    row = lax.broadcasted_iota(jnp.int32, (TILE, TILE), 0)
    col = lax.broadcasted_iota(jnp.int32, (TILE, TILE), 1)
    s_ref[:TILE, :] = jnp.where(row > col, s_ref[:TILE, :], NEG)
    s_ref[WINDOW:span, :] = jnp.where(row <= col, s_ref[WINDOW:span, :], NEG)

    @pl.when(rank_ref[0] == 0)
    def _():
        for c in range(WINDOW // TILE):
            @pl.when(c + t < WINDOW // TILE)
            def _():
                s_ref[c * TILE : (c + 1) * TILE, :] = jnp.full((TILE, TILE), NEG, F32)

    for half in range(halves):
        used = count_ref[t * halves + half]
        for e in range(1, TOPK):
            @pl.when(e >= used)
            def _():
                s_ref[
                    span + e * BLOCK : span + (e + 1) * BLOCK, half * BLOCK : (half + 1) * BLOCK
                ] = jnp.full((BLOCK, BLOCK), NEG, F32)

    steps = total // BLOCK

    def chunk(c):
        return pl.ds(pl.multiple_of(c * BLOCK, BLOCK), BLOCK)

    def fold(x, op):
        return op(x.reshape(BLOCK // 8, 8, TILE), 0)

    def top_step(c, top):
        return jnp.maximum(top, fold(s_ref[chunk(c), :], jnp.max))

    top = lax.fori_loop(0, steps, top_step, jnp.full((8, TILE), NEG, F32), unroll=2)
    top = jnp.max(top, 0, keepdims=True) * to_two

    def exp_step(c, acc):
        e = jnp.exp2(s_ref[chunk(c), :] * to_two - top)
        s_ref[chunk(c), :] = e
        return acc + fold(e, jnp.sum)

    acc = lax.fori_loop(0, steps, exp_step, jnp.zeros((8, TILE), F32), unroll=2)
    inv = 1.0 / jnp.sum(acc, 0, keepdims=True)

    def prob_step(c, acc):
        p = s_ref[chunk(c), :] * inv
        s_ref[chunk(c), :] = p
        p_ref[chunk(c), :] = p.astype(BF16)
        return acc + fold(p * dp_ref[chunk(c), :], jnp.sum)

    acc = lax.fori_loop(0, steps, prob_step, jnp.zeros((8, TILE), F32), unroll=2)
    delta = jnp.sum(acc, 0, keepdims=True)

    def score_step(c, carry):
        ds_ref[chunk(c), :] = (s_ref[chunk(c), :] * (dp_ref[chunk(c), :] - delta)).astype(BF16)
        return carry

    lax.fori_loop(0, steps, score_step, 0, unroll=2)

    o = dot(p_ref[:span, :], vx[win, :], TN)
    dq = dot(ds_ref[:span, :], kx[win, :], TN)
    for half in range(halves):
        cols = slice(half * BLOCK, (half + 1) * BLOCK)
        o_ref[0, cols, :] = (o[cols] + dot(p_ref[span:, cols], vm[half], TN)).astype(BF16)
        dq_ref[0, cols, :] = (
            scale * (dq[cols] + dot(ds_ref[span:, cols], km[half], TN))
        ).astype(BF16)
    va[win, :] += dot(p_ref[:span, :], g)
    ka[win, :] += dot(ds_ref[:span, :], q)

    @pl.when(t == pl.num_programs(1) - 1)
    def _():
        back_ref[0, 0] = (scale * ka[:WINDOW, :]).astype(BF16)
        back_ref[1, 0] = va[:WINDOW, :].astype(BF16)
        keep_ref[0, 0] = scale * ka[WINDOW:, :]
        keep_ref[1, 0] = va[WINDOW:, :]


def attend(slots, counts, rank, q, g, own, halo, mem, first):
    group, tokens = own.shape[1], own.shape[2]
    n_slots = mem.shape[0]
    tiles = tokens // TILE
    span = WINDOW + TILE
    total = span + TOPK * BLOCK
    halves = TILE // BLOCK
    whole = pl.BlockSpec((1, tokens, 128), lambda i, t, *_: (first + i, 0, 0))
    pair = pl.BlockSpec((2, 1, tokens, 128), lambda i, t, *_: (0, i, 0, 0))
    tile = pl.BlockSpec((1, TILE, 128), lambda i, t, *_: (i, t, 0))
    pairs = group * tiles * total * TILE
    return pl.pallas_call(
        attend_body,
        grid_spec=pltpu.PrefetchScalarGridSpec(
            num_scalar_prefetch=3,
            grid=(group, tiles),
            in_specs=[
                whole, whole, pair, pair,
                pl.BlockSpec((n_slots, 2, 1, BLOCK, 128), lambda i, t, *_: (0, 0, i, 0, 0)),
            ],
            out_specs=[tile, tile, pair, pair],
            scratch_shapes=[
                pltpu.VMEM((2 * WINDOW, 128), BF16),
                pltpu.VMEM((2 * WINDOW, 128), BF16),
                pltpu.VMEM((halves, TOPK * BLOCK, 128), BF16),
                pltpu.VMEM((halves, TOPK * BLOCK, 128), BF16),
                pltpu.VMEM((total, TILE), F32),
                pltpu.VMEM((total, TILE), F32),
                pltpu.VMEM((total, TILE), BF16),
                pltpu.VMEM((total, TILE), BF16),
                pltpu.VMEM((2 * WINDOW, 128), F32),
                pltpu.VMEM((2 * WINDOW, 128), F32),
            ],
        ),
        out_shape=[
            jax.ShapeDtypeStruct((group, tokens, 128), BF16),
            jax.ShapeDtypeStruct((group, tokens, 128), BF16),
            jax.ShapeDtypeStruct((2, group, tokens, 128), BF16),
            jax.ShapeDtypeStruct((2, group, tokens, 128), F32),
        ],
        compiler_params=pltpu.CompilerParams(vmem_limit_bytes=VMEM),
        cost_estimate=pl.CostEstimate(
            flops=pairs * 128 * 12, bytes_accessed=group * 6 * 2**20, transcendentals=pairs
        ),
        name="attend",
    )(slots, counts, rank, q, g, own, halo, mem)


def join_body(heads, group, n_groups, *refs):
    o_refs, dq_refs = refs[:n_groups], refs[n_groups : 2 * n_groups]
    keep_refs, back_refs = refs[2 * n_groups : 3 * n_groups], refs[3 * n_groups : 4 * n_groups]
    o_out, dq_out, dk_out, dv_out = refs[4 * n_groups :]
    perm = heads_to_rows(256, heads)
    per = 256 // heads

    def stack(pieces):
        return jnp.concatenate(pieces, 0)

    for part in range(o_out.shape[0] // 256):
        src = slice(part * per, (part + 1) * per)
        dst = slice(part * 256, (part + 1) * 256)
        hs = range(heads)
        o = stack([o_refs[h // group][h % group, src, :] for h in hs])
        dq = stack([dq_refs[h // group][h % group, src, :] for h in hs])
        both = dot(perm, jnp.concatenate([o, dq], 1)).astype(BF16)
        o_out[dst, :] = both[:, :128]
        dq_out[dst, :] = both[:, 128:]
        sums = []
        for kv in range(2):
            sums.append(
                stack(
                    [
                        (
                            keep_refs[h // group][kv, h % group, src, :]
                            + back_refs[h // group][kv, h % group, src, :].astype(F32)
                        ).astype(BF16)
                        for h in hs
                    ]
                )
            )
        both = dot(perm, jnp.concatenate(sums, 1)).astype(BF16)
        dk_out[dst, :] = both[:, :128]
        dv_out[dst, :] = both[:, 128:]


def join_heads(o, dq, keep, back, heads, group):
    n_groups = heads // group
    tokens = o[0].shape[1]
    steps = 4
    hm = pl.BlockSpec((group, tokens // steps, 128), lambda i: (0, i, 0))
    kv = pl.BlockSpec((2, group, tokens // steps, 128), lambda i: (0, 0, i, 0))
    out = pl.BlockSpec((tokens * heads // steps, 128), lambda i: (i, 0))
    return pl.pallas_call(
        functools.partial(join_body, heads, group, n_groups),
        grid=(steps,),
        in_specs=[hm] * (2 * n_groups) + [kv] * (2 * n_groups),
        out_specs=[out] * 4,
        out_shape=[jax.ShapeDtypeStruct((tokens * heads, 128), BF16)] * 4,
        cost_estimate=pl.CostEstimate(
            flops=4 * 2 * tokens * heads * 256 * 128,
            bytes_accessed=24 * tokens * heads * 128,
            transcendentals=0,
        ),
        compiler_params=pltpu.CompilerParams(vmem_limit_bytes=VMEM),
        name="join_heads",
    )(*o, *dq, *keep, *back)


def passed_along(block, axis, distance):
    devices = range(lax.axis_size(axis))
    route = [(i - distance, i) for i in devices if i - distance in devices]
    return lax.ppermute(block, axis, route)


def after(value, earlier):
    return lax.optimization_barrier((value, earlier))


def tables(mem_blocks, mem_count, mem_local, owners):
    packed = jnp.concatenate([mem_blocks, mem_count[:, None]], 1)
    every = lax.all_gather(packed, ("seq", "head"), axis=0, tiled=True)
    me = lax.axis_index("seq")
    rows = every.shape[0] // owners
    entries = rows * TOPK
    ids = every[:, :TOPK].reshape(owners, entries)
    count = every[:, TOPK].reshape(owners, rows)
    used = (
        jnp.arange(TOPK, dtype=jnp.int32)[None, None, :] < count[:, :, None]
    ).reshape(owners, entries)
    owner = ids // mem_local
    inside = ids % mem_local
    earlier = (
        jnp.arange(entries, dtype=jnp.int32)[None, :] < jnp.arange(entries, dtype=jnp.int32)[:, None]
    )
    same = (owner[:, :, None] == owner[:, None, :]) & used[:, None, :] & earlier[None]
    order = jnp.sum(same.astype(jnp.int32), 2)
    wanted = (
        (used & (owner == me))[:, :, None]
        & (order[:, :, None] == jnp.arange(LIVE, dtype=jnp.int32)[None, None, :])
    )
    send = jnp.sum(jnp.where(wanted, inside[:, :, None], 0), 1).reshape(owners * LIVE)
    slot = jnp.where(used, owner * LIVE + order, 0)
    pick = jnp.arange(owners, dtype=jnp.int32) == me
    mine = jnp.sum(jnp.where(pick[:, None], slot, 0), 0).reshape(rows, TOPK)
    my_count = jnp.sum(jnp.where(pick[:, None], count, 0), 0)
    live = jnp.arange(TOPK, dtype=jnp.int32)[None, :] < my_count[:, None]
    mine = jnp.where(live, mine, mine[:, :1]).reshape(entries)
    return send, mine, my_count, me.reshape(1)


def shards(queries, seg_keys, seg_values, mem_keys, mem_values, mem_blocks, mem_count, grad_out):
    tokens, heads, dim = queries.shape
    owners = lax.axis_size("seq")
    mem_local = mem_keys.shape[0] // BLOCK
    group = GROUP
    n_groups = heads // group

    def as_rows(x):
        return x.reshape(x.shape[0] * heads, dim)

    q, g, *own = split_heads(
        as_rows(queries), as_rows(grad_out), as_rows(seg_keys), as_rows(seg_values), heads, group
    )
    halo = [passed_along(x, "seq", 1) for x in own]
    (mem_blocks, mem_count), _ = after((mem_blocks, mem_count), q)
    send, slots, counts, rank = tables(mem_blocks, mem_count, mem_local, owners)
    picked = pick_blocks(
        send,
        mem_keys.reshape(mem_local, BLOCK * heads, dim),
        mem_values.reshape(mem_local, BLOCK * heads, dim),
        heads,
        group,
    )
    o, dq, keep, back = [], [], [], []
    got = []

    def fetch(i, *earlier):
        x, _ = after(picked[i], (halo[i], *earlier))
        x = x.reshape(owners, LIVE, 2, group, BLOCK, dim)
        x = lax.all_to_all(x, "seq", split_axis=0, concat_axis=0, tiled=True)
        got.append(x.reshape(owners * LIVE, 2, group, BLOCK, dim))

    fetch(0)
    for i in range(n_groups):
        if i + 1 < n_groups:
            fetch(i + 1, got[i], *back[: max(i - 1, 0)])
        parts = attend(slots, counts, rank, q, g, own[i], halo[i], got[i], i * group)
        o.append(parts[0])
        dq.append(parts[1])
        keep.append(parts[3])
        back.append(passed_along(parts[2], "seq", -1))
    outs = join_heads(o, dq, keep, back, heads, group)
    return tuple(x.reshape(tokens, heads, dim) for x in outs)


def solution(mesh):
    wide = P("seq", "head", None)
    return jax.shard_map(
        shards,
        mesh=mesh,
        in_specs=(wide, wide, wide, wide, wide, P(("seq", "head"), None), P(("seq", "head")), wide),
        out_specs=(wide, wide, wide, wide),
        check_vma=False,
    )
```

time: 739 us -> 290 us (0.39); the launches traced: 730 us -> 290 us
  local copies, waits for them, and re-layouts: 291 us -> 8.54 us
  matrix products: 132 us -> 0 us
  Pallas kernels: 0 us -> 86 us
  waiting for transfers between devices: 170 us -> 104 us
  blocking collectives: 84.4 us -> 36.8 us
  starting transfers between devices: 18.7 us -> 51.6 us
  other arithmetic: 33.1 us -> 1.37 us
    dynamic_update_slice x12 -> x0, local copies, waits for them, and re-layouts: 221 us -> none  [the longest x8 220 us: shards(): lax.map(backward_head, (queries_major, grads_major, keys_major, values_ma...]
    dot_general x72 -> x0, matrix products: 132 us -> none  [the longest x8 18.2 us: mix(): jnp.einsum('twj,tjd->twd', lower_w, key_tiles[:-1], preferred_element_typ...]
    pallas_call x0 -> x7, Pallas kernels: none -> 86 us  [the longest x4 62.9 us: attend(): pl.pallas_call(attend_body, grid_spec=pltpu.PrefetchScalarGridSpec(num_sc...]
    all_to_all x2 -> x0, blocking collectives: 66.4 us -> none  [the longest x1 52.8 us: fetch_memory(): lax.all_to_all(jnp.take(value_blocks, wanted, axis=0), 'seq', split_axis=...]
    ppermute x4 -> x8, waiting for transfers between devices: 170 us -> 104 us  [passed_along(): return lax.ppermute(block, axis, route)]
    gather x8 -> x0, local copies, waits for them, and re-layouts: 44.6 us -> none  [the longest x2 13.2 us: fetch_memory(): jnp.take(value_blocks, wanted, axis=0)]
    all_gather x1, blocking collectives: 8.52 us -> 36.8 us  [tables(): every = lax.all_gather(packed, ('seq', 'head'), axis=0, tiled=True)]
    reduce_sum x13 -> x4, other arithmetic: 21.1 us -> 0.76 us  [the longest x1 0.46 us: tables(): order = jnp.sum(same.astype(jnp.int32), 2)]
  transfers between devices with their start and end apart: 5 -> 12, of which waited for: 4 -> 4; matrix products, arithmetic and copies ran while one was open for 3% -> 1% of each run, Pallas kernels for 0% -> 26%
where the time goes in v1:
time: 290 us
  waiting for transfers between devices  104 us (36%)
  Pallas kernels  86 us (30%)
  starting transfers between devices  51.6 us (18%)
  blocking collectives  36.8 us (13%)
  local copies, waits for them, and re-layouts  8.54 us (3%)
    ppermute x8, waiting for transfers between devices, passed_along(): return lax.ppermute(block, axis, route)  104 us
    pallas_call x4, Pallas kernels, attend(): pl.pallas_call(attend_body, grid_spec=pltpu.PrefetchScalarGridSpec(num_sc...  62.9 us
    all_gather x1, blocking collectives, tables(): every = lax.all_gather(packed, ('seq', 'head'), axis=0, tiled=True)  36.8 us
    all_to_all x4, starting transfers between devices, fetch(): x = lax.all_to_all(x, 'seq', split_axis=0, concat_axis=0, tiled=True)  27.6 us
    ppermute x8, starting transfers between devices, passed_along(): return lax.ppermute(block, axis, route)  24 us
    pallas_call x1, Pallas kernels, pick_blocks(): pl.pallas_call(functools.partial(pick_body, heads, group, per_step), grid...  11.1 us
    unnamed x28, local copies, waits for them, and re-layouts  6.75 us
    pallas_call x1, Pallas kernels, join_heads(): pl.pallas_call(functools.partial(join_body, heads, group, n_groups), grid...  6.46 us
  transfers between devices with their start and end apart: 12, of which 4 were waited for; matrix products, arithmetic and copies ran while one was open for 1% of the time, Pallas kernels for 26%

profile of v1, /device:TPU:6, one launch (start us, length us, event | category | flops | bytes accessed | tf_op | source)
XLA Modules:
  0.0 289.5 jit_solution(6689547648441870035)
XLA Ops:
  0.6 5.5 %split_heads.1 = (bf16[4,1024,128]{2,1,0:T(8,128)(2,1)}, bf16[4,1024,128]{2,1,0:T(8,128)(2,1)}, bf16[2,1,1024,128]{3,2,1,0:T(8,128)(2,1)}, bf16[2,1,1024,128]{3,...) custom-call(bf16[4096,128]{1,0:T(8,128)(2,1)} %bitcast.47, ...), custom_call_target="tpu_custom_call" | custom-call | flops 1073741824 | bytes 8388608 | tf_op jit(solution)/shard_map/split_heads/pallas_call | solution.py:69
  6.2 3.7 %collective-permute-start = (bf16[2,1,1024,128]{3,2,1,0:T(8,128)(2,1)}, bf16[2,1,1024,128]{3,2,1,0:T(8,128)(2,1)S(1)}, u32[]{:S(2)}, u32[]{:S(2)}) collective-permute-start(bf16[2,1,1024,128]{3,2,1,0:T(8,128)(2,1)} %get-tuple-element.44.own_ref), channel_id=1, source_target_pairs={{0,8},{8,16},{16,24},{24,32},{32,40},{40,48},{48,56},{56,64},{64,7... | collective-permute-start | bytes 1572872 | tf_op jit(solution)/shard_map/ppermute | solution.py:361
  10.6 0.1 add_bitcast_fusion
  10.7 36.8 %all-gather = s32[128,1,5]{2,1,0:T(1,128)S(1)} all-gather(s32[1,1,5]{2,1,0:T(1,128)S(1)} %add_bitcast_fusion), channel_id=1, replica_groups=mesh['seq'=16,'head'=8] {'seq','head'}, dimensions={0}, use_global_device_ids=true | all-gather | bytes 2580 | tf_op jit(solution)/shard_map/all_gather | solution.py:370
  47.4 0.2 slice_reduce_fusion
  47.6 0.1 reshape.263
  47.7 0.1 reshape_squeeze.3
  47.8 0.1 copy.38
  47.9 0.1 lt.74
  48.0 0.5 convert_reduce_fusion
  48.5 0.1 select_reduce_fusion
  48.6 0.1 copy.40
  48.7 0.6 reshape.265.idx_ref
  49.3 11.1 %pick_blocks.1 = (bf16[32,2,1,128,128]{4,3,2,1,0:T(8,128)(2,1)}, bf16[32,2,1,128,128]{4,3,2,1,0:T(8,128)(2,1)}, bf16[32,2,1,128,128]{4,3,2,1,0:T(8,128)(2,1)}, bf16[32,2,1,128,128]{4,3,2,1,0:T(8,128)(2,1)}) custom-call(s32[32]{0:T(128)} %reshape.265.idx_ref, bf16[32,512,128]{2,1,0:T(8,128)(2,1)} %bitcast.34, bf16[32,512,128]{2,1,0:T(8,128)(2,1)} %bitcast.38, ...), custom_call_target="tpu_custom_call" | custom-call | flops 2147483648 | bytes 16777216 | tf_op jit(solution)/shard_map/pick_blocks/pallas_call | solution.py:114
  60.5 0.8 copy-done.11
  61.2 7.1 %all-to-all-start = ((bf16[16,2,2,1,128,128]{5,4,2,1,3,0:T(8,128)(2,1)}), bf16[16,2,2,1,128,128]{5,4,2,1,3,0:T(8,128)(2,1)S(1)}, u32[]{:S(2)}, u32[]{:S(2)}) async-start(bf16[16,2,2,1,128,128]{5,4,2,1,3,0:T(8,128)(2,1)} %bitcast.46), calls=%async_computation | async-start | bytes 4194304 | tf_op jit(solution)/shard_map/all_to_all | solution.py:429
  68.4 3.4 %collective-permute-start.1 = (bf16[2,1,1024,128]{3,2,1,0:T(8,128)(2,1)S(1)}, bf16[2,1,1024,128]{3,2,1,0:T(8,128)(2,1)}, u32[]{:S(2)}, u32[]{:S(2)}) collective-permute-start(bf16[2,1,1024,128]{3,2,1,0:T(8,128)(2,1)S(1)} %copy-done.10), channel_id=1, source_target_pairs={{0,8},{8,16},{16,24},{24,32},{32,40},{40,48},{48,56},{56,64},{64,7... | collective-permute-start | bytes 1572872 | tf_op jit(solution)/shard_map/ppermute | solution.py:361
  71.7 37.8 %collective-permute-done.1.halo_ref = bf16[2,1,1024,128]{3,2,1,0:T(8,128)(2,1)} collective-permute-done((bf16[2,1,1024,128]{3,2,1,0:T(8,128)(2,1)S(1)}, bf16[2,1,1024,128]{3,2,1,0:T(8,128)(2,1)}, u32[]{:S(2)}, u32[]{:S(2)}) %collective-permute-start.1) | collective-permute-done | bytes 524320 | tf_op jit(solution)/shard_map/ppermute | solution.py:361
  109.5 1.4 copy-done.1
  110.9 6.8 %all-to-all-start.1 = ((bf16[16,2,2,1,128,128]{5,4,2,1,3,0:T(8,128)(2,1)}), bf16[16,2,2,1,128,128]{5,4,2,1,3,0:T(8,128)(2,1)S(1)}, u32[]{:S(2)}, u32[]{:S(2)}) async-start(bf16[16,2,2,1,128,128]{5,4,2,1,3,0:T(8,128)(2,1)} %bitcast.45), calls=%async_computation.1 | async-start | bytes 4194304 | tf_op jit(solution)/shard_map/all_to_all | solution.py:429
  117.7 3.4 %collective-permute-start.2 = (bf16[2,1,1024,128]{3,2,1,0:T(8,128)(2,1)S(1)}, bf16[2,1,1024,128]{3,2,1,0:T(8,128)(2,1)}, u32[]{:S(2)}, u32[]{:S(2)}) collective-permute-start(bf16[2,1,1024,128]{3,2,1,0:T(8,128)(2,1)S(1)} %copy-done.9), channel_id=1, source_target_pairs={{0,8},{8,16},{16,24},{24,32},{32,40},{40,48},{48,56},{56,64},{64,7... | collective-permute-start | bytes 1572872 | tf_op jit(solution)/shard_map/ppermute | solution.py:361
  121.1 34.6 %collective-permute-done.2.halo_ref = bf16[2,1,1024,128]{3,2,1,0:T(8,128)(2,1)} collective-permute-done((bf16[2,1,1024,128]{3,2,1,0:T(8,128)(2,1)S(1)}, bf16[2,1,1024,128]{3,2,1,0:T(8,128)(2,1)}, u32[]{:S(2)}, u32[]{:S(2)}) %collective-permute-start.2) | collective-permute-done | bytes 524320 | tf_op jit(solution)/shard_map/ppermute | solution.py:361
  155.7 1.4 copy-done
  157.1 7.0 %all-to-all-start.2 = ((bf16[16,2,2,1,128,128]{5,4,2,1,3,0:T(8,128)(2,1)}), bf16[16,2,2,1,128,128]{5,4,2,1,3,0:T(8,128)(2,1)}, u32[]{:S(2)}, u32[]{:S(2)}) async-start(bf16[16,2,2,1,128,128]{5,4,2,1,3,0:T(8,128)(2,1)} %bitcast.18), calls=%async_computation.2 | async-start | bytes 4194304 | tf_op jit(solution)/shard_map/all_to_all | solution.py:429
  164.1 3.4 %collective-permute-start.3 = (bf16[2,1,1024,128]{3,2,1,0:T(8,128)(2,1)S(1)}, bf16[2,1,1024,128]{3,2,1,0:T(8,128)(2,1)S(1)}, u32[]{:S(2)}, u32[]{:S(2)}) collective-permute-start(bf16[2,1,1024,128]{3,2,1,0:T(8,128)(2,1)S(1)} %copy-done.8), channel_id=1, source_target_pairs={{0,8},{8,16},{16,24},{24,32},{32,40},{40,48},{48,56},{56,64},{64,7... | collective-permute-start | bytes 1572872 | tf_op jit(solution)/shard_map/ppermute | solution.py:361
  167.5 0.1 select_reduce_fusion.1
  167.6 0.1 reduce_sum.41
  167.7 0.1 slice_reduce_fusion.1
  167.9 0.1 broadcast_in_dim.71
  168.0 0.1 select_reduce_fusion.2.count_ref
  168.1 0.1 lt.76
  168.2 0.5 compare_select_fusion.slot_ref
  168.7 15.7 %attend.4 = (bf16[1,1024,128]{2,1,0:T(8,128)(2,1)}, bf16[1,1024,128]{2,1,0:T(8,128)(2,1)}, bf16[2,1,1024,128]{3,2,1,0:T(8,128)(2,1)}, f32[2,1,1024,128]{3,2,1,0:T(8,128)}) custom-call(s32[32]{0:T(128)} %compare_select_fusion.slot_ref, s32[8]{0:T(128)} %copy-done.7, s32[1]{0:T(128)} %bitcast.8.rank_ref, bf16[4,1024,128]{2,1,0:T(8,128)(2,1)} %get-tuple-element.40.q_ref, ...), custom_call_target="tpu_custom_call" | custom-call | flops 2818572288 | bytes 6291456 | tf_op jit(solution)/shard_map/attend/pallas_call | solution.py:261
  184.4 2.5 collective-permute-start.4
  186.9 17.2 %collective-permute-done.3.halo_ref = bf16[2,1,1024,128]{3,2,1,0:T(8,128)(2,1)S(1)} collective-permute-done((bf16[2,1,1024,128]{3,2,1,0:T(8,128)(2,1)S(1)}, bf16[2,1,1024,128]{3,2,1,0:T(8,128)(2,1)S(1)}, u32[]{:S(2)}, u32[]{:S(2)}) %collective-permute-start.3) | collective-permute-done | bytes 524320 | tf_op jit(solution)/shard_map/ppermute | solution.py:361
  204.1 0.8 copy-done.12
  204.9 0.2 copy-done.3
  205.2 6.7 %all-to-all-start.3 = ((bf16[16,2,2,1,128,128]{5,4,2,1,3,0:T(8,128)(2,1)}), bf16[16,2,2,1,128,128]{5,4,2,1,3,0:T(8,128)(2,1)S(1)}, u32[]{:S(2)}, u32[]{:S(2)}) async-start(bf16[16,2,2,1,128,128]{5,4,2,1,3,0:T(8,128)(2,1)} %bitcast.21), calls=%async_computation.3 | async-start | bytes 4194304 | tf_op jit(solution)/shard_map/all_to_all | solution.py:429
  211.8 15.7 %attend.5 = (bf16[1,1024,128]{2,1,0:T(8,128)(2,1)}, bf16[1,1024,128]{2,1,0:T(8,128)(2,1)}, bf16[2,1,1024,128]{3,2,1,0:T(8,128)(2,1)}, f32[2,1,1024,128]{3,2,1,0:T(8,128)}) custom-call(s32[32]{0:T(128)} %compare_select_fusion.slot_ref, s32[8]{0:T(128)} %copy-done.7, s32[1]{0:T(128)} %bitcast.8.rank_ref, bf16[4,1024,128]{2,1,0:T(8,128)(2,1)} %get-tuple-element.40.q_ref, ...), custom_call_target="tpu_custom_call" | custom-call | flops 2818572288 | bytes 6291456 | tf_op jit(solution)/shard_map/attend/pallas_call | solution.py:261
  227.6 2.8 collective-permute-start.5
  230.3 15.8 %attend.6 = (bf16[1,1024,128]{2,1,0:T(8,128)(2,1)}, bf16[1,1024,128]{2,1,0:T(8,128)(2,1)}, bf16[2,1,1024,128]{3,2,1,0:T(8,128)(2,1)}, f32[2,1,1024,128]{3,2,1,0:T(8,128)}) custom-call(s32[32]{0:T(128)} %compare_select_fusion.slot_ref, s32[8]{0:T(128)} %copy-done.7, s32[1]{0:T(128)} %bitcast.8.rank_ref, bf16[4,1024,128]{2,1,0:T(8,128)(2,1)} %get-tuple-element.40.q_ref, ...), custom_call_target="tpu_custom_call" | custom-call | flops 2818572288 | bytes 6291456 | tf_op jit(solution)/shard_map/attend/pallas_call | solution.py:261
  246.1 2.7 collective-permute-start.6
  248.8 1.3 copy-done.2
  250.1 15.7 %attend.7 = (bf16[1,1024,128]{2,1,0:T(8,128)(2,1)}, bf16[1,1024,128]{2,1,0:T(8,128)(2,1)}, bf16[2,1,1024,128]{3,2,1,0:T(8,128)(2,1)}, f32[2,1,1024,128]{3,2,1,0:T(8,128)}) custom-call(s32[32]{0:T(128)} %compare_select_fusion.slot_ref, s32[8]{0:T(128)} %copy-done.7, s32[1]{0:T(128)} %bitcast.8.rank_ref, bf16[4,1024,128]{2,1,0:T(8,128)(2,1)} %get-tuple-element.40.q_ref, ...), custom_call_target="tpu_custom_call" | custom-call | flops 2818572288 | bytes 6291456 | tf_op jit(solution)/shard_map/attend/pallas_call | solution.py:261
  265.8 2.2 collective-permute-start.7
  268.1 14.0 %collective-permute-done.7.refs_15_ = bf16[2,1,1024,128]{3,2,1,0:T(8,128)(2,1)S(1)} collective-permute-done((bf16[2,1,1024,128]{3,2,1,0:T(8,128)(2,1)}, bf16[2,1,1024,128]{3,2,1,0:T(8,128)(2,1)S(1)}, u32[]{:S(2)}, u32[]{:S(2)}) %collective-permute-start.7) | collective-permute-done | bytes 524320 | tf_op jit(solution)/shard_map/ppermute | solution.py:361
  282.1 0.8 copy-done.6
  282.9 6.5 %join_heads.1 = (bf16[4096,128]{1,0:T(8,128)(2,1)}, bf16[4096,128]{1,0:T(8,128)(2,1)}, bf16[4096,128]{1,0:T(8,128)(2,1)}, bf16[4096,128]{1,0:T(8,128)(2,1)}) custom-call(bf16[1,1024,128]{2,1,0:T(8,128)(2,1)} %get-tuple-element.47.refs_0_, bf16[1,1024,128]{2,1,0:T(8,128)(2,1)} %get-tuple-element.51.refs_1_, bf16[1,1024,128]{2,1,0:T(8,128)(2,1)} %get-tuple-element.55.refs_2_, ...), custom_call_target="tpu_custom_call" | custom-call | flops 1073741824 | bytes 12582912 | tf_op jit(solution)/shard_map/join_heads/pallas_call | solution.py:342
  (38 shorter events, 0.3 us)
Async XLA Ops:
  0.6 9.9 %copy-start.13 = (s32[1,4]{1,0:T(1,128)S(1)}, s32[1,4]{1,0:T(1,128)}, u32[]{:S(2)}) copy-start(s32[1,4]{1,0:T(1,128)} %param.13) | copy-start | bytes 52
  6.2 54.3 %collective-permute-start = (bf16[2,1,1024,128]{3,2,1,0:T(8,128)(2,1)}, bf16[2,1,1024,128]{3,2,1,0:T(8,128)(2,1)S(1)}, u32[]{:S(2)}, u32[]{:S(2)}) collective-permute-start(bf16[2,1,1024,128]{3,2,1,0:T(8,128)(2,1)} %get-tuple-element.44.own_ref), channel_id=1, source_target_pairs={{0,8},{8,16},{16,24},{24,32},{32,40},{40,48},{48,56},{56,64},{64,7... | collective-permute-start | bytes 1572872 | tf_op jit(solution)/shard_map/ppermute | solution.py:361
  60.4 0.8 copy-start.11
  60.4 7.9 %copy-start.10 = (bf16[2,1,1024,128]{3,2,1,0:T(8,128)(2,1)S(1)}, bf16[2,1,1024,128]{3,2,1,0:T(8,128)(2,1)}, u32[]{:S(2)}) copy-start(bf16[2,1,1024,128]{3,2,1,0:T(8,128)(2,1)} %get-tuple-element.48.own_ref) | copy-start | bytes 1572868
  61.2 48.3 %all-to-all-start = ((bf16[16,2,2,1,128,128]{5,4,2,1,3,0:T(8,128)(2,1)}), bf16[16,2,2,1,128,128]{5,4,2,1,3,0:T(8,128)(2,1)S(1)}, u32[]{:S(2)}, u32[]{:S(2)}) async-start(bf16[16,2,2,1,128,128]{5,4,2,1,3,0:T(8,128)(2,1)} %bitcast.46), calls=%async_computation | async-start | bytes 4194304 | tf_op jit(solution)/shard_map/all_to_all | solution.py:429
  68.4 41.2 %collective-permute-start.1 = (bf16[2,1,1024,128]{3,2,1,0:T(8,128)(2,1)S(1)}, bf16[2,1,1024,128]{3,2,1,0:T(8,128)(2,1)}, u32[]{:S(2)}, u32[]{:S(2)}) collective-permute-start(bf16[2,1,1024,128]{3,2,1,0:T(8,128)(2,1)S(1)} %copy-done.10), channel_id=1, source_target_pairs={{0,8},{8,16},{16,24},{24,32},{32,40},{40,48},{48,56},{56,64},{64,7... | collective-permute-start | bytes 1572872 | tf_op jit(solution)/shard_map/ppermute | solution.py:361
  109.5 1.4 copy-start.1
  109.5 8.2 %copy-start.9 = (bf16[2,1,1024,128]{3,2,1,0:T(8,128)(2,1)S(1)}, bf16[2,1,1024,128]{3,2,1,0:T(8,128)(2,1)}, u32[]{:S(2)}) copy-start(bf16[2,1,1024,128]{3,2,1,0:T(8,128)(2,1)} %get-tuple-element.52.own_ref) | copy-start | bytes 1572868
  110.9 44.8 %all-to-all-start.1 = ((bf16[16,2,2,1,128,128]{5,4,2,1,3,0:T(8,128)(2,1)}), bf16[16,2,2,1,128,128]{5,4,2,1,3,0:T(8,128)(2,1)S(1)}, u32[]{:S(2)}, u32[]{:S(2)}) async-start(bf16[16,2,2,1,128,128]{5,4,2,1,3,0:T(8,128)(2,1)} %bitcast.45), calls=%async_computation.1 | async-start | bytes 4194304 | tf_op jit(solution)/shard_map/all_to_all | solution.py:429
  117.7 38.0 %collective-permute-start.2 = (bf16[2,1,1024,128]{3,2,1,0:T(8,128)(2,1)S(1)}, bf16[2,1,1024,128]{3,2,1,0:T(8,128)(2,1)}, u32[]{:S(2)}, u32[]{:S(2)}) collective-permute-start(bf16[2,1,1024,128]{3,2,1,0:T(8,128)(2,1)S(1)} %copy-done.9), channel_id=1, source_target_pairs={{0,8},{8,16},{16,24},{24,32},{32,40},{40,48},{48,56},{56,64},{64,7... | collective-permute-start | bytes 1572872 | tf_op jit(solution)/shard_map/ppermute | solution.py:361
  155.7 1.4 copy-start
  155.7 8.4 %copy-start.8 = (bf16[2,1,1024,128]{3,2,1,0:T(8,128)(2,1)S(1)}, bf16[2,1,1024,128]{3,2,1,0:T(8,128)(2,1)}, u32[]{:S(2)}) copy-start(bf16[2,1,1024,128]{3,2,1,0:T(8,128)(2,1)} %get-tuple-element.56.own_ref) | copy-start | bytes 1572868
  157.1 47.1 %all-to-all-start.2 = ((bf16[16,2,2,1,128,128]{5,4,2,1,3,0:T(8,128)(2,1)}), bf16[16,2,2,1,128,128]{5,4,2,1,3,0:T(8,128)(2,1)}, u32[]{:S(2)}, u32[]{:S(2)}) async-start(bf16[16,2,2,1,128,128]{5,4,2,1,3,0:T(8,128)(2,1)} %bitcast.18), calls=%async_computation.2 | async-start | bytes 4194304 | tf_op jit(solution)/shard_map/all_to_all | solution.py:429
  164.1 40.0 %collective-permute-start.3 = (bf16[2,1,1024,128]{3,2,1,0:T(8,128)(2,1)S(1)}, bf16[2,1,1024,128]{3,2,1,0:T(8,128)(2,1)S(1)}, u32[]{:S(2)}, u32[]{:S(2)}) collective-permute-start(bf16[2,1,1024,128]{3,2,1,0:T(8,128)(2,1)S(1)} %copy-done.8), channel_id=1, source_target_pairs={{0,8},{8,16},{16,24},{24,32},{32,40},{40,48},{48,56},{56,64},{64,7... | collective-permute-start | bytes 1572872 | tf_op jit(solution)/shard_map/ppermute | solution.py:361
  168.0 0.7 copy-start.7
  184.4 19.7 %collective-permute-start.4 = (bf16[2,1,1024,128]{3,2,1,0:T(8,128)(2,1)}, bf16[2,1,1024,128]{3,2,1,0:T(8,128)(2,1)S(1)}, u32[]{:S(2)}, u32[]{:S(2)}) collective-permute-start(bf16[2,1,1024,128]{3,2,1,0:T(8,128)(2,1)} %get-tuple-element.58), channel_id=1, source_target_pairs={{8,0},{16,8},{24,16},{32,24},{40,32},{48,40},{56,48},{64,56},{72,6... | collective-permute-start | bytes 1572872 | tf_op jit(solution)/shard_map/ppermute | solution.py:361
  204.1 0.8 copy-start.12
  204.1 1.1 copy-start.3
  205.2 43.6 %all-to-all-start.3 = ((bf16[16,2,2,1,128,128]{5,4,2,1,3,0:T(8,128)(2,1)}), bf16[16,2,2,1,128,128]{5,4,2,1,3,0:T(8,128)(2,1)S(1)}, u32[]{:S(2)}, u32[]{:S(2)}) async-start(bf16[16,2,2,1,128,128]{5,4,2,1,3,0:T(8,128)(2,1)} %bitcast.21), calls=%async_computation.3 | async-start | bytes 4194304 | tf_op jit(solution)/shard_map/all_to_all | solution.py:429
  227.6 40.5 %collective-permute-start.5 = (bf16[2,1,1024,128]{3,2,1,0:T(8,128)(2,1)}, bf16[2,1,1024,128]{3,2,1,0:T(8,128)(2,1)S(1)}, u32[]{:S(2)}, u32[]{:S(2)}) collective-permute-start(bf16[2,1,1024,128]{3,2,1,0:T(8,128)(2,1)} %get-tuple-element.69), channel_id=1, source_target_pairs={{8,0},{16,8},{24,16},{32,24},{40,32},{48,40},{56,48},{64,56},{72,6... | collective-permute-start | bytes 1572872 | tf_op jit(solution)/shard_map/ppermute | solution.py:361
  246.1 22.0 %collective-permute-start.6 = (bf16[2,1,1024,128]{3,2,1,0:T(8,128)(2,1)}, bf16[2,1,1024,128]{3,2,1,0:T(8,128)(2,1)S(1)}, u32[]{:S(2)}, u32[]{:S(2)}) collective-permute-start(bf16[2,1,1024,128]{3,2,1,0:T(8,128)(2,1)} %get-tuple-element.70), channel_id=1, source_target_pairs={{8,0},{16,8},{24,16},{32,24},{40,32},{48,40},{56,48},{64,56},{72,6... | collective-permute-start | bytes 1572872 | tf_op jit(solution)/shard_map/ppermute | solution.py:361
  248.8 1.3 copy-start.2
  265.8 16.3 %collective-permute-start.7 = (bf16[2,1,1024,128]{3,2,1,0:T(8,128)(2,1)}, bf16[2,1,1024,128]{3,2,1,0:T(8,128)(2,1)S(1)}, u32[]{:S(2)}, u32[]{:S(2)}) collective-permute-start(bf16[2,1,1024,128]{3,2,1,0:T(8,128)(2,1)} %get-tuple-element.71), channel_id=1, source_target_pairs={{8,0},{16,8},{24,16},{32,24},{40,32},{48,40},{56,48},{64,56},{72,6... | collective-permute-start | bytes 1572872 | tf_op jit(solution)/shard_map/ppermute | solution.py:361
  268.1 14.0 %copy-start.4 = (bf16[2,1,1024,128]{3,2,1,0:T(8,128)(2,1)}, bf16[2,1,1024,128]{3,2,1,0:T(8,128)(2,1)S(1)}, u32[]{:S(2)}) copy-start(bf16[2,1,1024,128]{3,2,1,0:T(8,128)(2,1)S(1)} %collective-permute-done.5.refs_13_) | copy-start | bytes 1572868
  268.1 14.0 %copy-start.5 = (bf16[2,1,1024,128]{3,2,1,0:T(8,128)(2,1)}, bf16[2,1,1024,128]{3,2,1,0:T(8,128)(2,1)S(1)}, u32[]{:S(2)}) copy-start(bf16[2,1,1024,128]{3,2,1,0:T(8,128)(2,1)S(1)} %collective-permute-done.6.refs_14_) | copy-start | bytes 1572868
  282.1 0.8 copy-start.6

commit v2 on v1

v2 whole, which is shorter than its diff:
```python
import functools
import math

import jax
import jax.numpy as jnp
from jax import lax
from jax.experimental import pallas as pl
from jax.experimental.pallas import tpu as pltpu
from jax.sharding import PartitionSpec as P

WINDOW = 1024
BLOCK = 128
TOPK = 4
LIVE = 2
TILE = 256
VMEM = 58 * 1024 * 1024
NEG = -1e30
F32 = jnp.float32
BF16 = jnp.bfloat16
NT = (((1,), (1,)), ((), ()))
TN = (((0,), (0,)), ((), ()))


def rows_to_heads(rows, heads):
    out = lax.broadcasted_iota(jnp.int32, (rows, rows), 0)
    src = lax.broadcasted_iota(jnp.int32, (rows, rows), 1)
    per = rows // heads
    return (src == heads * (out % per) + out // per).astype(BF16)


def heads_to_rows(rows, heads):
    out = lax.broadcasted_iota(jnp.int32, (rows, rows), 0)
    src = lax.broadcasted_iota(jnp.int32, (rows, rows), 1)
    per = rows // heads
    return (src == per * (out % heads) + out // heads).astype(BF16)


def dot(a, b, dims=None):
    if dims is None:
        return jnp.dot(a, b, preferred_element_type=F32)
    return lax.dot_general(a, b, dims, preferred_element_type=F32)


def split_heads_body(heads, q_ref, d_ref, k_ref, v_ref, qo_ref, do_ref, kv_ref):
    perm = rows_to_heads(256, heads)
    per = 256 // heads
    for part in range(q_ref.shape[0] // 256):
        src = pl.ds(part * 256, 256)
        dst = pl.ds(part * per, per)
        qd = dot(perm, jnp.concatenate([q_ref[src, :], d_ref[src, :]], 1)).astype(BF16)
        kv = dot(perm, jnp.concatenate([k_ref[src, :], v_ref[src, :]], 1)).astype(BF16)
        for h in range(heads):
            rows = slice(h * per, (h + 1) * per)
            qo_ref[h, dst, :] = qd[rows, :128]
            do_ref[h, dst, :] = qd[rows, 128:]
            kv_ref[h, 0, dst, :] = kv[rows, :128]
            kv_ref[h, 1, dst, :] = kv[rows, 128:]


def split_heads(q, d, k, v, heads):
    rows = q.shape[0]
    tokens = rows // heads
    steps = 4
    in_spec = pl.BlockSpec((rows // steps, 128), lambda i: (i, 0))
    hm = pl.BlockSpec((heads, tokens // steps, 128), lambda i: (0, i, 0))
    kv = pl.BlockSpec((heads, 2, tokens // steps, 128), lambda i: (0, 0, i, 0))
    return pl.pallas_call(
        functools.partial(split_heads_body, heads),
        grid=(steps,),
        in_specs=[in_spec] * 4,
        out_specs=[hm, hm, kv],
        out_shape=[jax.ShapeDtypeStruct((heads, tokens, 128), BF16)] * 2
        + [jax.ShapeDtypeStruct((heads, 2, tokens, 128), BF16)],
        cost_estimate=pl.CostEstimate(
            flops=4 * 2 * rows * 256 * 128, bytes_accessed=16 * rows * 128, transcendentals=0
        ),
        compiler_params=pltpu.CompilerParams(vmem_limit_bytes=VMEM),
        name="split_heads",
    )(q, d, k, v)


def pick_body(heads, per_step, idx_ref, *refs):
    ins, out = refs[: 2 * per_step], refs[2 * per_step]
    perm = rows_to_heads(256, heads)
    per = 256 // heads
    for j in range(per_step):
        k_ref, v_ref = ins[2 * j], ins[2 * j + 1]
        for part in range(BLOCK * heads // 256):
            src = pl.ds(part * 256, 256)
            dst = pl.ds(part * per, per)
            kv = dot(perm, jnp.concatenate([k_ref[0, src, :], v_ref[0, src, :]], 1)).astype(BF16)
            for h in range(heads):
                rows = slice(h * per, (h + 1) * per)
                out[h, j, 0, dst, :] = kv[rows, :128]
                out[h, j, 1, dst, :] = kv[rows, 128:]


def pick_blocks(index, mem_k, mem_v, heads):
    slots = index.shape[0]
    per_step = 4

    def at(j):
        return pl.BlockSpec(
            (1, BLOCK * heads, 128), lambda i, idx, j=j: (idx[i * per_step + j], 0, 0)
        )

    ins = []
    for _ in range(per_step):
        ins += [mem_k, mem_v]
    return pl.pallas_call(
        functools.partial(pick_body, heads, per_step),
        grid_spec=pltpu.PrefetchScalarGridSpec(
            num_scalar_prefetch=1,
            grid=(slots // per_step,),
            in_specs=[at(j // 2) for j in range(2 * per_step)],
            out_specs=pl.BlockSpec((heads, per_step, 2, BLOCK, 128), lambda i, idx: (0, i, 0, 0, 0)),
        ),
        out_shape=jax.ShapeDtypeStruct((heads, slots, 2, BLOCK, 128), BF16),
        compiler_params=pltpu.CompilerParams(vmem_limit_bytes=VMEM),
        cost_estimate=pl.CostEstimate(
            flops=slots * 4 * BLOCK * heads * 256 * 128,
            bytes_accessed=slots * 8 * BLOCK * heads * 128,
            transcendentals=0,
        ),
        name="pick_blocks",
    )(index, *ins)


def attend_tile(refs, t, rank, h, ka, va):
    (slot_ref, count_ref, q_ref, g_ref, o_ref, dq_ref, cur, kx, vx, km, vm, s_ref, dp_ref, p_ref, ds_ref) = refs
    span = WINDOW + TILE
    total = span + TOPK * BLOCK
    halves = TILE // BLOCK
    scale = 1.0 / math.sqrt(128.0)
    to_two = scale * math.log2(math.e)
    start = pl.multiple_of(t * TILE, TILE)
    win = pl.ds(start, span)
    q = q_ref[h, pl.ds(start, TILE), :]
    g = g_ref[h, pl.ds(start, TILE), :]

    for half in range(halves):
        for e in range(TOPK):
            slot = slot_ref[(t * halves + half) * TOPK + e]
            km[half, e * BLOCK : (e + 1) * BLOCK, :] = cur[slot, 0]
            vm[half, e * BLOCK : (e + 1) * BLOCK, :] = cur[slot, 1]

    s_ref[:span, :] = dot(kx[win, :], q, NT)
    dp_ref[:span, :] = dot(vx[win, :], g, NT)
    for half in range(halves):
        cols = slice(half * BLOCK, (half + 1) * BLOCK)
        used = count_ref[t * halves + half]
        far = dot(km[half], q[cols], NT)
        for e in range(TOPK):
            rows = slice(e * BLOCK, (e + 1) * BLOCK)
            s_ref[span + e * BLOCK : span + (e + 1) * BLOCK, cols] = jnp.where(
                e < used, far[rows], NEG
            )
        dp_ref[span:, cols] = dot(vm[half], g[cols], NT)

    row = lax.broadcasted_iota(jnp.int32, (TILE, TILE), 0)
    col = lax.broadcasted_iota(jnp.int32, (TILE, TILE), 1)
    s_ref[:TILE, :] = jnp.where(row > col, s_ref[:TILE, :], NEG)
    s_ref[WINDOW:span, :] = jnp.where(row <= col, s_ref[WINDOW:span, :], NEG)

    @pl.when(rank == 0)
    def _():
        for c in range(WINDOW // TILE):
            @pl.when(c + t < WINDOW // TILE)
            def _():
                s_ref[c * TILE : (c + 1) * TILE, :] = jnp.full((TILE, TILE), NEG, F32)

    steps = total // BLOCK

    def chunk(c):
        return pl.ds(pl.multiple_of(c * BLOCK, BLOCK), BLOCK)

    def fold(x, op):
        return op(x.reshape(BLOCK // 8, 8, TILE), 0)

    def top_step(c, top):
        return jnp.maximum(top, fold(s_ref[chunk(c), :], jnp.max))

    top = lax.fori_loop(0, steps, top_step, jnp.full((8, TILE), NEG, F32), unroll=2)
    top = jnp.max(top, 0, keepdims=True) * to_two

    def exp_step(c, acc):
        e = jnp.exp2(s_ref[chunk(c), :] * to_two - top)
        s_ref[chunk(c), :] = e
        return acc + fold(e, jnp.sum)

    acc = lax.fori_loop(0, steps, exp_step, jnp.zeros((8, TILE), F32), unroll=2)
    inv = 1.0 / jnp.sum(acc, 0, keepdims=True)

    def prob_step(c, acc):
        p = s_ref[chunk(c), :] * inv
        s_ref[chunk(c), :] = p
        p_ref[chunk(c), :] = p.astype(BF16)
        return acc + fold(p * dp_ref[chunk(c), :], jnp.sum)

    acc = lax.fori_loop(0, steps, prob_step, jnp.zeros((8, TILE), F32), unroll=2)
    delta = jnp.sum(acc, 0, keepdims=True)

    def score_step(c, carry):
        ds_ref[chunk(c), :] = (s_ref[chunk(c), :] * (dp_ref[chunk(c), :] - delta)).astype(BF16)
        return carry

    lax.fori_loop(0, steps, score_step, 0, unroll=2)

    o = dot(p_ref[:span, :], vx[win, :], TN)
    dq = dot(ds_ref[:span, :], kx[win, :], TN)
    for half in range(halves):
        cols = slice(half * BLOCK, (half + 1) * BLOCK)
        dst = pl.ds(pl.multiple_of(start + half * BLOCK, BLOCK), BLOCK)
        o_ref[h, dst, :] = (o[cols] + dot(p_ref[span:, cols], vm[half], TN)).astype(BF16)
        dq_ref[h, dst, :] = (
            scale * (dq[cols] + dot(ds_ref[span:, cols], km[half], TN))
        ).astype(BF16)
    va[win, :] += dot(p_ref[:span, :], g)
    ka[win, :] += dot(ds_ref[:span, :], q)


def exchange_body(
    heads, n, slot_ref, count_ref, q_ref, g_ref, own_ref, sent_ref, o_ref, dq_ref, dkv_ref,
    recv, halo, leave, back, cur, kx, vx, km, vm, s_ref, dp_ref, p_ref, ds_ref, ka, va,
    far_send, far_recv, near, halo_send, halo_recv, back_send, back_recv,
):
    me = lax.axis_index("seq")
    tiles = WINDOW // TILE
    scale = 1.0 / math.sqrt(128.0)
    barrier = pltpu.get_barrier_semaphore()

    def peer(r):
        return lax.rem(me + r, n)

    def greet(r, c):
        pl.semaphore_signal(barrier, inc=1, device_id={"seq": peer(r)})
        return c

    lax.fori_loop(1, n, greet, 0)
    pl.semaphore_wait(barrier, n - 1)

    def far_copy(h, r):
        return pltpu.make_async_remote_copy(
            src_ref=sent_ref.at[h, peer(r)],
            dst_ref=recv.at[h, me],
            send_sem=far_send.at[h, r],
            recv_sem=far_recv.at[h, r],
            device_id={"seq": peer(r)},
        )

    def near_copy(h):
        return pltpu.make_async_copy(sent_ref.at[h, me], recv.at[h, me], near.at[h])

    def halo_copy(h):
        return pltpu.make_async_remote_copy(
            src_ref=own_ref.at[h],
            dst_ref=halo.at[h],
            send_sem=halo_send.at[h],
            recv_sem=halo_recv.at[h],
            device_id={"seq": peer(1)},
        )

    def back_copy(h, t):
        return pltpu.make_async_remote_copy(
            src_ref=leave.at[h, t],
            dst_ref=back.at[h, t],
            send_sem=back_send.at[h, t],
            recv_sem=back_recv.at[h, t],
            device_id={"seq": peer(n - 1)},
        )

    def over(lo, hi, what):
        def step(i, c):
            what(i)
            return c

        lax.fori_loop(lo, hi, step, 0)

    def send_head(h):
        halo_copy(h).start()
        near_copy(h).start()
        over(1, n, lambda r: far_copy(h, r).start())

    def wait_head(h):
        halo_copy(h).wait_recv()
        near_copy(h).wait()
        over(1, n, lambda r: far_copy(h, r).wait_recv())

    def finish(h):
        odd = lax.rem(h, 2)

        def piece(t):
            back_copy(h, t).wait_recv()
            rows = pl.ds(pl.multiple_of(t * TILE, TILE), TILE)
            kept = pl.ds(pl.multiple_of(WINDOW + t * TILE, TILE), TILE)
            dkv_ref[h, 0, rows, :] = (
                scale * ka[odd, kept, :] + back[h, t, 0].astype(F32)
            ).astype(BF16)
            dkv_ref[h, 1, rows, :] = (va[odd, kept, :] + back[h, t, 1].astype(F32)).astype(BF16)

        over(0, tiles, piece)

    send_head(0)
    send_head(1)

    def head(h):
        wait_head(h)

        @pl.when(h + 2 < heads)
        def _():
            send_head(h + 2)

        odd = lax.rem(h, 2)

        def move(i):
            for s in range(LIVE):
                cur[i * LIVE + s] = recv[h, i, s]

        over(0, n, move)
        kx[:WINDOW, :] = halo[h, 0]
        kx[WINDOW:, :] = own_ref[h, 0]
        vx[:WINDOW, :] = halo[h, 1]
        vx[WINDOW:, :] = own_ref[h, 1]
        ka[odd] = jnp.zeros_like(ka[odd])
        va[odd] = jnp.zeros_like(va[odd])

        def tile(t):
            refs = (
                slot_ref, count_ref, q_ref, g_ref, o_ref, dq_ref, cur,
                kx, vx, km, vm, s_ref, dp_ref, p_ref, ds_ref,
            )
            attend_tile(refs, t, me, h, ka.at[odd], va.at[odd])
            rows = pl.ds(pl.multiple_of(t * TILE, TILE), TILE)
            leave[h, t, 0] = (scale * ka[odd, rows, :]).astype(BF16)
            leave[h, t, 1] = va[odd, rows, :].astype(BF16)
            back_copy(h, t).start()

        over(0, tiles, tile)

        @pl.when(h > 0)
        def _():
            finish(h - 1)

    over(0, heads, head)
    finish(heads - 1)

    def drain(h):
        halo_copy(h).wait_send()
        over(1, n, lambda r: far_copy(h, r).wait_send())
        over(0, tiles, lambda t: back_copy(h, t).wait_send())

    over(0, heads, drain)


def exchange(slots, counts, q, g, own, sent, n):
    heads, tokens = q.shape[:2]
    tiles = tokens // TILE
    span = WINDOW + TILE
    total = span + TOPK * BLOCK
    halves = TILE // BLOCK
    pairs = heads * tiles * total * TILE
    vmem = pl.BlockSpec(memory_space=pltpu.VMEM)
    smem = pl.BlockSpec(memory_space=pltpu.SMEM)
    hbm = pl.BlockSpec(memory_space=pl.ANY)
    dma = pltpu.SemaphoreType.DMA
    return pl.pallas_call(
        functools.partial(exchange_body, heads, n),
        in_specs=[smem, smem, vmem, vmem, vmem, hbm],
        out_specs=[vmem, vmem, vmem],
        out_shape=[
            jax.ShapeDtypeStruct(q.shape, BF16),
            jax.ShapeDtypeStruct(q.shape, BF16),
            jax.ShapeDtypeStruct((heads, 2, tokens, 128), BF16),
        ],
        scratch_shapes=[
            pltpu.VMEM((heads, n, LIVE, 2, BLOCK, 128), BF16),
            pltpu.VMEM((heads, 2, WINDOW, 128), BF16),
            pltpu.VMEM((heads, tiles, 2, TILE, 128), BF16),
            pltpu.VMEM((heads, tiles, 2, TILE, 128), BF16),
            pltpu.VMEM((n * LIVE, 2, BLOCK, 128), BF16),
            pltpu.VMEM((2 * WINDOW, 128), BF16),
            pltpu.VMEM((2 * WINDOW, 128), BF16),
            pltpu.VMEM((halves, TOPK * BLOCK, 128), BF16),
            pltpu.VMEM((halves, TOPK * BLOCK, 128), BF16),
            pltpu.VMEM((total, TILE), F32),
            pltpu.VMEM((total, TILE), F32),
            pltpu.VMEM((total, TILE), BF16),
            pltpu.VMEM((total, TILE), BF16),
            pltpu.VMEM((2, 2 * WINDOW, 128), F32),
            pltpu.VMEM((2, 2 * WINDOW, 128), F32),
            dma((heads, n)), dma((heads, n)), dma((heads,)),
            dma((heads,)), dma((heads,)), dma((heads, tiles)), dma((heads, tiles)),
        ],
        compiler_params=pltpu.CompilerParams(
            vmem_limit_bytes=VMEM, collective_id=0, has_side_effects=True
        ),
        cost_estimate=pl.CostEstimate(
            flops=pairs * 128 * 12, bytes_accessed=heads * 6 * 2**20, transcendentals=pairs
        ),
        name="exchange_attend",
    )(slots, counts, q, g, own, sent)


def share_body(n, m, row_ref, all_ref, near, mine, near_send, near_recv, far_send, far_recv):
    me = lax.axis_index("seq")
    hd = lax.axis_index("head")
    barrier = pltpu.get_barrier_semaphore()

    def over(lo, hi, what):
        def step(i, c):
            what(i)
            return c

        lax.fori_loop(lo, hi, step, 0)

    def far_peer(r):
        return {"seq": lax.rem(me + r, n)}

    def near_peer(r):
        return {"head": lax.rem(hd + r, m)}

    over(1, n, lambda r: pl.semaphore_signal(barrier, inc=1, device_id=far_peer(r)))
    over(1, m, lambda r: pl.semaphore_signal(barrier, inc=1, device_id=near_peer(r)))
    pl.semaphore_wait(barrier, n + m - 2)

    def near_copy(r):
        return pltpu.make_async_remote_copy(
            src_ref=row_ref,
            dst_ref=near.at[hd],
            send_sem=near_send.at[r],
            recv_sem=near_recv.at[r],
            device_id=near_peer(r),
        )

    def far_copy(r):
        return pltpu.make_async_remote_copy(
            src_ref=mine,
            dst_ref=all_ref.at[me],
            send_sem=far_send.at[r],
            recv_sem=far_recv.at[r],
            device_id=far_peer(r),
        )

    over(1, m, lambda r: near_copy(r).start())
    near[hd] = row_ref[...]
    over(1, m, lambda r: near_copy(r).wait_recv())
    for i in range(m):
        mine[i : i + 1, :] = near[i, 0:1, :]
    over(1, n, lambda r: far_copy(r).start())
    all_ref[me] = mine[...]
    over(1, n, lambda r: far_copy(r).wait_recv())
    over(1, m, lambda r: near_copy(r).wait_send())
    over(1, n, lambda r: far_copy(r).wait_send())


def share_rows(row, n, m):
    dma = pltpu.SemaphoreType.DMA
    vmem = pl.BlockSpec(memory_space=pltpu.VMEM)
    return pl.pallas_call(
        functools.partial(share_body, n, m),
        in_specs=[vmem],
        out_specs=vmem,
        out_shape=jax.ShapeDtypeStruct((n, m, 128), jnp.int32),
        scratch_shapes=[
            pltpu.VMEM((m, 8, 128), jnp.int32),
            pltpu.VMEM((m, 128), jnp.int32),
            dma((m,)), dma((m,)), dma((n,)), dma((n,)),
        ],
        compiler_params=pltpu.CompilerParams(collective_id=1, has_side_effects=True),
        name="share_rows",
    )(row)


def join_body(heads, o_ref, dq_ref, dkv_ref, o_out, dq_out, dk_out, dv_out):
    perm = heads_to_rows(256, heads)
    per = 256 // heads
    for part in range(o_out.shape[0] // 256):
        src = slice(part * per, (part + 1) * per)
        dst = slice(part * 256, (part + 1) * 256)
        o = jnp.concatenate([o_ref[h, src, :] for h in range(heads)], 0)
        dq = jnp.concatenate([dq_ref[h, src, :] for h in range(heads)], 0)
        both = dot(perm, jnp.concatenate([o, dq], 1)).astype(BF16)
        o_out[dst, :] = both[:, :128]
        dq_out[dst, :] = both[:, 128:]
        dk = jnp.concatenate([dkv_ref[h, 0, src, :] for h in range(heads)], 0)
        dv = jnp.concatenate([dkv_ref[h, 1, src, :] for h in range(heads)], 0)
        both = dot(perm, jnp.concatenate([dk, dv], 1)).astype(BF16)
        dk_out[dst, :] = both[:, :128]
        dv_out[dst, :] = both[:, 128:]


def join_heads(o, dq, dkv):
    heads, tokens = o.shape[:2]
    steps = 4
    hm = pl.BlockSpec((heads, tokens // steps, 128), lambda i: (0, i, 0))
    kv = pl.BlockSpec((heads, 2, tokens // steps, 128), lambda i: (0, 0, i, 0))
    out = pl.BlockSpec((tokens * heads // steps, 128), lambda i: (i, 0))
    return pl.pallas_call(
        functools.partial(join_body, heads),
        grid=(steps,),
        in_specs=[hm, hm, kv],
        out_specs=[out] * 4,
        out_shape=[jax.ShapeDtypeStruct((tokens * heads, 128), BF16)] * 4,
        compiler_params=pltpu.CompilerParams(vmem_limit_bytes=VMEM),
        cost_estimate=pl.CostEstimate(
            flops=4 * 2 * tokens * heads * 256 * 128,
            bytes_accessed=16 * tokens * heads * 128,
            transcendentals=0,
        ),
        name="join_heads",
    )(o, dq, dkv)


def tables(mem_blocks, mem_count, mem_local, owners):
    packed = jnp.concatenate([mem_blocks, mem_count[:, None]], 1)
    packed = jnp.broadcast_to(jnp.pad(packed, ((0, 0), (0, 128 - packed.shape[1]))), (8, 128))
    every = share_rows(packed, owners, lax.axis_size("head")).reshape(-1, 128)
    me = lax.axis_index("seq")
    rows = every.shape[0] // owners
    entries = rows * TOPK
    ids = every[:, :TOPK].reshape(owners, entries)
    count = every[:, TOPK].reshape(owners, rows)
    used = (
        jnp.arange(TOPK, dtype=jnp.int32)[None, None, :] < count[:, :, None]
    ).reshape(owners, entries)
    owner = ids // mem_local
    inside = ids % mem_local
    earlier = (
        jnp.arange(entries, dtype=jnp.int32)[None, :] < jnp.arange(entries, dtype=jnp.int32)[:, None]
    )
    same = (owner[:, :, None] == owner[:, None, :]) & used[:, None, :] & earlier[None]
    order = jnp.sum(same.astype(jnp.int32), 2)
    wanted = (
        (used & (owner == me))[:, :, None]
        & (order[:, :, None] == jnp.arange(LIVE, dtype=jnp.int32)[None, None, :])
    )
    send = jnp.sum(jnp.where(wanted, inside[:, :, None], 0), 1).reshape(owners * LIVE)
    slot = jnp.where(used, owner * LIVE + order, 0)
    pick = jnp.arange(owners, dtype=jnp.int32) == me
    mine = jnp.sum(jnp.where(pick[:, None], slot, 0), 0).reshape(rows, TOPK)
    my_count = jnp.sum(jnp.where(pick[:, None], count, 0), 0)
    live = jnp.arange(TOPK, dtype=jnp.int32)[None, :] < my_count[:, None]
    mine = jnp.where(live, mine, mine[:, :1]).reshape(entries)
    return send, mine, my_count


def shards(queries, seg_keys, seg_values, mem_keys, mem_values, mem_blocks, mem_count, grad_out):
    tokens, heads, dim = queries.shape
    owners = lax.axis_size("seq")
    mem_local = mem_keys.shape[0] // BLOCK

    def as_rows(x):
        return x.reshape(x.shape[0] * heads, dim)

    send, slots, counts = tables(mem_blocks, mem_count, mem_local, owners)
    q, g, own = split_heads(
        as_rows(queries), as_rows(grad_out), as_rows(seg_keys), as_rows(seg_values), heads
    )
    sent = pick_blocks(
        send,
        mem_keys.reshape(mem_local, BLOCK * heads, dim),
        mem_values.reshape(mem_local, BLOCK * heads, dim),
        heads,
    )
    sent = sent.reshape(heads, owners, LIVE, 2, BLOCK, dim)
    outs = join_heads(*exchange(slots, counts, q, g, own, sent, owners))
    return tuple(x.reshape(tokens, heads, dim) for x in outs)


def solution(mesh):
    wide = P("seq", "head", None)
    return jax.shard_map(
        shards,
        mesh=mesh,
        in_specs=(wide, wide, wide, wide, wide, P(("seq", "head"), None), P(("seq", "head")), wide),
        out_specs=(wide, wide, wide, wide),
        check_vma=False,
    )
```

time: 290 us -> 222 us (0.77)
  Pallas kernels: 86 us -> 214 us
  waiting for transfers between devices: 104 us -> 0 us
  starting transfers between devices: 51.6 us -> 0 us
  blocking collectives: 36.8 us -> 0 us
  local copies, waits for them, and re-layouts: 8.54 us -> 4.09 us
    pallas_call x7 -> x5, Pallas kernels: 86 us -> 214 us  [the longest x1 176 us: exchange(): pl.pallas_call(functools.partial(exchange_body, heads, n), in_specs=[smem...]
    ppermute x8 -> x0, waiting for transfers between devices: 104 us -> none  [passed_along(): return lax.ppermute(block, axis, route)]
    all_gather x1 -> x0, blocking collectives: 36.8 us -> none  [tables(): every = lax.all_gather(packed, ('seq', 'head'), axis=0, tiled=True)]
    all_to_all x4 -> x0, starting transfers between devices: 27.6 us -> none  [fetch(): x = lax.all_to_all(x, 'seq', split_axis=0, concat_axis=0, tiled=True)]
    ppermute x8 -> x0, starting transfers between devices: 24 us -> none  [passed_along(): return lax.ppermute(block, axis, route)]
    unnamed x28 -> x2, local copies, waits for them, and re-layouts: 6.75 us -> 0.01 us
  transfers between devices with their start and end apart: 12 -> 0, of which waited for: 4 -> 0; matrix products, arithmetic and copies ran while one was open for 1% -> 0% of each run, Pallas kernels for 26% -> 0%
where the time goes in v2:
time: 222 us
  Pallas kernels  214 us (96%)
  local copies, waits for them, and re-layouts  4.09 us (2%)
    pallas_call x1, Pallas kernels, exchange(): pl.pallas_call(functools.partial(exchange_body, heads, n), in_specs=[smem...  176 us
    pallas_call x1, Pallas kernels, share_rows(): pl.pallas_call(functools.partial(share_body, n, m), in_specs=[vmem], out_...  16.4 us
    pallas_call x1, Pallas kernels, pick_blocks(): pl.pallas_call(functools.partial(pick_body, heads, per_step), grid_spec=p...  11.1 us
    pallas_call x1, Pallas kernels, join_heads(): pl.pallas_call(functools.partial(join_body, heads), grid=(steps,), in_spe...  5.52 us
    pallas_call x1, Pallas kernels, split_heads(): pl.pallas_call(functools.partial(split_heads_body, heads), grid=(steps,),...  5.51 us

profile of v2, /device:TPU:6, one launch (start us, length us, event | category | flops | bytes accessed | tf_op | source)
XLA Modules:
  0.0 221.6 jit_solution(9535723372165676770)
XLA Ops:
  1.3 0.7 pad_add_fusion
  2.0 0.6 broadcast_in_dim.75.row_ref
  2.6 0.1 lt.74
  2.7 16.4 %share_rows.1 = s32[16,8,128]{2,1,0:T(8,128)} custom-call(s32[8,128]{1,0:T(8,128)} %broadcast_in_dim.75.row_ref), custom_call_target="tpu_custom_call" | custom-call | tf_op jit(solution)/shard_map/share_rows/pallas_call | solution.py:459
  19.1 1.0 slice_reduce_fusion
  20.1 0.1 reshape_squeeze.3
  20.2 0.1 select_reduce_fusion.2.count_ref
  20.3 0.0 copy-start
  20.4 0.1 copy.24
  20.4 0.1 lt.75
  20.5 0.1 lt.76
  20.6 0.9 reshape.239
  21.5 0.1 copy.25
  21.6 0.5 convert_reduce_fusion
  22.1 0.1 select_reduce_fusion.1
  22.2 0.1 select_reduce_fusion
  22.3 0.1 reduce_sum.41
  22.4 0.1 slice_reduce_fusion.1
  22.5 0.1 broadcast_in_dim.79
  22.6 0.1 broadcast_in_dim.80
  22.6 0.5 compare_select_fusion.slot_ref
  23.2 0.1 copy.26
  23.3 0.7 reshape.244.idx_ref
  23.9 5.5 %split_heads.1 = (bf16[4,1024,128]{2,1,0:T(8,128)(2,1)}, bf16[4,1024,128]{2,1,0:T(8,128)(2,1)}, bf16[4,2,1024,128]{3,2,1,0:T(8,128)(2,1)}) custom-call(bf16[4096,128]{1,0:T(8,128)(2,1)} %bitcast.27, bf16[4096,128]{1,0:T(8,128)(2,1)} %bitcast.28, bf16[4096,128]{1,0:T(8,128)(2,1)} %bitcast.29, bf16[4096,128]{1,0:T(8,128)(2,1)} %bitcast.30), custom_call_target="tpu_custom_call" | custom-call | flops 1073741824 | bytes 8388608 | tf_op jit(solution)/shard_map/split_heads/pallas_call | solution.py:67
  29.4 11.1 %pick_blocks.1 = bf16[4,32,2,128,128]{4,3,2,1,0:T(8,128)(2,1)} custom-call(s32[32]{0:T(128)} %reshape.244.idx_ref, bf16[32,512,128]{2,1,0:T(8,128)(2,1)} %bitcast.18, bf16[32,512,128]{2,1,0:T(8,128)(2,1)} %bitcast.22, bf16[32,512,128]{2,1,0:T(8,128)(2,1)} %bitcast.19, bf16[32,512,128]{2,1,0:T(8,128)(2,1)} %bitcast.23, bf16[32,512,128]{2,1,0:T(8,128)(2,1)} %bitcast.20, ...), custom_call_target="tpu_custom_call" | custom-call | flops 2147483648 | bytes 16777216 | tf_op jit(solution)/shard_map/pick_blocks/pallas_call | solution.py:110
  40.5 0.0 copy-done
  40.5 175.5 %exchange_attend.1 = (bf16[4,1024,128]{2,1,0:T(8,128)(2,1)}, bf16[4,1024,128]{2,1,0:T(8,128)(2,1)}, bf16[4,2,1024,128]{3,2,1,0:T(8,128)(2,1)}) custom-call(s32[32]{0:T(128)} %compare_select_fusion.slot_ref, s32[8]{0:T(128)} %copy-done, bf16[4,1024,128]{2,1,0:T(8,128)(2,1)} %get-tuple-element.14.q_ref, bf16[4,1024,128]{2,1,0:T(8,128)(2,1)} %get-tuple-element.15.g_ref, ...), custom_call_target="tpu_custom_call" | custom-call | flops 11274289152 | bytes 25165824 | tf_op jit(solution)/shard_map/exchange_attend/pallas_call | solution.py:366
  216.1 5.5 %join_heads.1 = (bf16[4096,128]{1,0:T(8,128)(2,1)}, bf16[4096,128]{1,0:T(8,128)(2,1)}, bf16[4096,128]{1,0:T(8,128)(2,1)}, bf16[4096,128]{1,0:T(8,128)(2,1)}) custom-call(bf16[4,1024,128]{2,1,0:T(8,128)(2,1)} %get-tuple-element.17.o_ref, bf16[4,1024,128]{2,1,0:T(8,128)(2,1)} %get-tuple-element.18.dq_ref, bf16[4,2,1024,128]{3,2,1,0:T(8,128)(2,1)} %get-tuple-element.19.dkv_ref), custom_call_target="tpu_custom_call" | custom-call | flops 1073741824 | bytes 8388608 | tf_op jit(solution)/shard_map/join_heads/pallas_call | solution.py:498
  (7 shorter events, 0.1 us)
Async XLA Ops:
  20.3 20.2 %copy-start = (s32[8]{0:T(128)}, s32[8]{0:T(128)S(1)}, u32[]{:S(2)}) copy-start(s32[8]{0:T(128)S(1)} %select_reduce_fusion.2.count_ref) | copy-start | bytes 100

commit v3 on v2

v3 whole, which is shorter than its diff:
```python
import functools
import math

import jax
import jax.numpy as jnp
from jax import lax
from jax.experimental import pallas as pl
from jax.experimental.pallas import tpu as pltpu
from jax.sharding import PartitionSpec as P

WINDOW = 1024
BLOCK = 128
TOPK = 4
LIVE = 2
MEM_DEV = 32
QB_DEV = 8
SIDE = 4
ORDER = (
    (2, 2), (1, 2), (2, 1), (3, 2), (2, 3), (0, 2), (2, 0),
    (1, 1), (3, 3), (1, 3), (3, 1), (0, 1), (0, 3), (1, 0), (3, 0),
)
TILE = 256
VMEM = 60 * 1024 * 1024
NEG = -1e30
F32 = jnp.float32
BF16 = jnp.bfloat16
NT = (((1,), (1,)), ((), ()))
TN = (((0,), (0,)), ((), ()))


def rows_to_heads(rows, heads):
    out = lax.broadcasted_iota(jnp.int32, (rows, rows), 0)
    src = lax.broadcasted_iota(jnp.int32, (rows, rows), 1)
    per = rows // heads
    return (src == heads * (out % per) + out // per).astype(BF16)


def heads_to_rows(rows, heads):
    out = lax.broadcasted_iota(jnp.int32, (rows, rows), 0)
    src = lax.broadcasted_iota(jnp.int32, (rows, rows), 1)
    per = rows // heads
    return (src == per * (out % heads) + out // heads).astype(BF16)


def dot(a, b, dims=None):
    if dims is None:
        return jnp.dot(a, b, preferred_element_type=F32)
    return lax.dot_general(a, b, dims, preferred_element_type=F32)


def attend_tile(refs, t, rank, h, ka, va):
    (plan_s, q_ref, g_ref, o_ref, dq_ref, cur, kx, vx, km, vm, s_ref, dp_ref, p_ref, ds_ref) = refs
    span = WINDOW + TILE
    total = span + TOPK * BLOCK
    halves = TILE // BLOCK
    scale = 1.0 / math.sqrt(128.0)
    to_two = scale * math.log2(math.e)
    start = pl.multiple_of(t * TILE, TILE)
    win = pl.ds(start, span)
    q = q_ref[h, pl.ds(start, TILE), :]
    g = g_ref[h, pl.ds(start, TILE), :]

    for half in range(halves):
        for e in range(TOPK):
            slot = plan_s[LIVE, rank, (t * halves + half) * TOPK + e]
            first = plan_s[LIVE, rank, (t * halves + half) * TOPK]
            slot = jnp.maximum(jnp.where(slot < 0, first, slot), 0)
            km[half, e * BLOCK : (e + 1) * BLOCK, :] = cur[slot, 0]
            vm[half, e * BLOCK : (e + 1) * BLOCK, :] = cur[slot, 1]

    s_ref[:span, :] = dot(kx[win, :], q, NT)
    dp_ref[:span, :] = dot(vx[win, :], g, NT)
    for half in range(halves):
        cols = slice(half * BLOCK, (half + 1) * BLOCK)
        far = dot(km[half], q[cols], NT)
        for e in range(TOPK):
            rows = slice(e * BLOCK, (e + 1) * BLOCK)
            s_ref[span + e * BLOCK : span + (e + 1) * BLOCK, cols] = jnp.where(
                plan_s[LIVE, rank, (t * halves + half) * TOPK + e] >= 0, far[rows], NEG
            )
        dp_ref[span:, cols] = dot(vm[half], g[cols], NT)

    row = lax.broadcasted_iota(jnp.int32, (TILE, TILE), 0)
    col = lax.broadcasted_iota(jnp.int32, (TILE, TILE), 1)
    s_ref[:TILE, :] = jnp.where(row > col, s_ref[:TILE, :], NEG)
    s_ref[WINDOW:span, :] = jnp.where(row <= col, s_ref[WINDOW:span, :], NEG)

    @pl.when(rank == 0)
    def _():
        for c in range(WINDOW // TILE):
            @pl.when(c + t < WINDOW // TILE)
            def _():
                s_ref[c * TILE : (c + 1) * TILE, :] = jnp.full((TILE, TILE), NEG, F32)

    steps = total // BLOCK

    def chunk(c):
        return pl.ds(pl.multiple_of(c * BLOCK, BLOCK), BLOCK)

    def fold(x, op):
        return op(x.reshape(BLOCK // 8, 8, TILE), 0)

    def top_step(c, top):
        return jnp.maximum(top, fold(s_ref[chunk(c), :], jnp.max))

    top = lax.fori_loop(0, steps, top_step, jnp.full((8, TILE), NEG, F32), unroll=2)
    top = jnp.max(top, 0, keepdims=True) * to_two

    def exp_step(c, acc):
        e = jnp.exp2(s_ref[chunk(c), :] * to_two - top)
        s_ref[chunk(c), :] = e
        return acc + fold(e, jnp.sum)

    acc = lax.fori_loop(0, steps, exp_step, jnp.zeros((8, TILE), F32), unroll=2)
    inv = 1.0 / jnp.sum(acc, 0, keepdims=True)

    def prob_step(c, acc):
        p = s_ref[chunk(c), :] * inv
        s_ref[chunk(c), :] = p
        p_ref[chunk(c), :] = p.astype(BF16)
        return acc + fold(p * dp_ref[chunk(c), :], jnp.sum)

    acc = lax.fori_loop(0, steps, prob_step, jnp.zeros((8, TILE), F32), unroll=2)
    delta = jnp.sum(acc, 0, keepdims=True)

    def score_step(c, carry):
        ds_ref[chunk(c), :] = (s_ref[chunk(c), :] * (dp_ref[chunk(c), :] - delta)).astype(BF16)
        return carry

    lax.fori_loop(0, steps, score_step, 0, unroll=2)

    o = dot(p_ref[:span, :], vx[win, :], TN)
    dq = dot(ds_ref[:span, :], kx[win, :], TN)
    for half in range(halves):
        cols = slice(half * BLOCK, (half + 1) * BLOCK)
        dst = pl.ds(pl.multiple_of(start + half * BLOCK, BLOCK), BLOCK)
        o_ref[h, dst, :] = (o[cols] + dot(p_ref[span:, cols], vm[half], TN)).astype(BF16)
        dq_ref[h, dst, :] = (
            scale * (dq[cols] + dot(ds_ref[span:, cols], km[half], TN))
        ).astype(BF16)
    va[win, :] += dot(p_ref[:span, :], g)
    ka[win, :] += dot(ds_ref[:span, :], q)


def exchange_body(
    heads, n, m, ids_ref, used_ref, q_hbm, g_hbm, k_hbm, v_hbm, mk_hbm, mv_hbm,
    o_ref, dq_ref, dkv_ref,
    raw, mem, q_ref, g_ref, own_ref, sent_ref, near_tab, my_tab, far_tab, flat, plan, plan_s,
    recv, halo, leave, back, cur, kx, vx, km, vm, s_ref, dp_ref, p_ref, ds_ref, ka, va,
    load_sem, plan_sem, tab_near_send, tab_near_recv, tab_far_send, tab_far_recv,
    far_send, far_recv, near, halo_send, halo_recv, back_send, back_recv,
):
    me = lax.axis_index("seq")
    hd = lax.axis_index("head")
    tiles = WINDOW // TILE
    scale = 1.0 / math.sqrt(128.0)
    barrier = pltpu.get_barrier_semaphore()

    def over(lo, hi, what, unroll=None):
        def step(i, c):
            what(i)
            return c

        lax.fori_loop(lo, hi, step, 0, unroll=unroll)

    def peer(r):
        return lax.rem(me + r, n)

    def shifted(k):
        dz, dx = ORDER[k]
        return lax.rem(me // SIDE + dz, SIDE) * SIDE + lax.rem(lax.rem(me, SIDE) + dx, SIDE)

    def head_peer(r):
        return {"head": lax.rem(hd + r, m)}

    loads = [
        pltpu.make_async_copy(src, raw.at[i], load_sem.at[i])
        for i, src in enumerate((k_hbm, v_hbm, q_hbm, g_hbm))
    ] + [
        pltpu.make_async_copy(src, mem.at[i], load_sem.at[4 + i])
        for i, src in enumerate((mk_hbm, mv_hbm))
    ]
    for load in loads:
        load.start()

    over(1, n, lambda r: pl.semaphore_signal(barrier, inc=1, device_id={"seq": peer(r)}))
    over(1, m, lambda r: pl.semaphore_signal(barrier, inc=1, device_id=head_peer(r)))

    lane = lax.broadcasted_iota(jnp.int32, (8, 128), 1)
    row = jnp.zeros((8, 128), jnp.int32)
    for e in range(TOPK):
        value = jnp.where(e < used_ref[0], ids_ref[0, e] + 1, 0)
        row = jnp.where(lane == hd * TOPK + e, value, row)
    near_tab[hd] = row
    pl.semaphore_wait(barrier, n + m - 2)

    def tab_near(r):
        return pltpu.make_async_remote_copy(
            src_ref=near_tab.at[hd],
            dst_ref=near_tab.at[hd],
            send_sem=tab_near_send.at[r],
            recv_sem=tab_near_recv.at[r],
            device_id=head_peer(r),
        )

    def tab_far(r):
        return pltpu.make_async_remote_copy(
            src_ref=my_tab,
            dst_ref=far_tab.at[me],
            send_sem=tab_far_send.at[r],
            recv_sem=tab_far_recv.at[r],
            device_id={"seq": peer(r)},
        )

    def far_copy(h, k):
        return pltpu.make_async_remote_copy(
            src_ref=sent_ref.at[h, shifted(k)],
            dst_ref=recv.at[h, me],
            send_sem=far_send.at[h, k],
            recv_sem=far_recv.at[h, k],
            device_id={"seq": shifted(k)},
        )

    def near_copy(h):
        return pltpu.make_async_copy(sent_ref.at[h, me], recv.at[h, me], near.at[h])

    def halo_copy(h):
        return pltpu.make_async_remote_copy(
            src_ref=own_ref.at[h],
            dst_ref=halo.at[h],
            send_sem=halo_send.at[h],
            recv_sem=halo_recv.at[h],
            device_id={"seq": peer(1)},
        )

    def back_copy(h, t):
        return pltpu.make_async_remote_copy(
            src_ref=leave.at[h, t],
            dst_ref=back.at[h, t],
            send_sem=back_send.at[h, t],
            recv_sem=back_recv.at[h, t],
            device_id={"seq": peer(n - 1)},
        )

    over(1, m, lambda r: tab_near(r).start())

    perm = rows_to_heads(256, heads)
    per = 256 // heads

    def split(left, right, left_out, right_out):
        both = dot(perm, jnp.concatenate([left, right], 1)).astype(BF16)
        for h in range(heads):
            left_out(h, both[h * per : (h + 1) * per, :128])
            right_out(h, both[h * per : (h + 1) * per, 128:])

    def put(ref, *at):
        def store(h, x):
            ref[(h, *at)] = x

        return store

    def spans(i):
        return (
            pl.ds(pl.multiple_of(i * 256, 256), 256),
            pl.ds(pl.multiple_of(i * per, per), per),
        )

    def split_kv(i):
        src, dst = spans(i)
        split(raw[0, src, :], raw[1, src, :], put(own_ref, 0, dst), put(own_ref, 1, dst))

    def split_qg(i):
        src, dst = spans(i)
        split(raw[2, src, :], raw[3, src, :], put(q_ref, dst), put(g_ref, dst))

    parts = WINDOW * heads // 256
    loads[0].wait()
    loads[1].wait()
    over(0, parts, split_kv, unroll=2)
    halo_copy(0).start()
    halo_copy(1).start()

    over(1, m, lambda r: tab_near(r).wait_recv())
    total = near_tab[0]
    for i in range(1, m):
        total = total + near_tab[i]
    my_tab[...] = total
    far_tab[me] = total
    over(1, n, lambda r: tab_far(r).start())

    loads[2].wait()
    loads[3].wait()
    over(0, parts, split_qg, unroll=2)
    over(1, n, lambda r: tab_far(r).wait_recv())

    for d in range(n):
        flat[d : d + 1, :] = far_tab[d, 0:1, :]
    table = flat[...] - 1
    owner = lax.shift_right_arithmetic(table, 5)
    inside = lax.bitwise_and(table, MEM_DEV - 1)
    live = table >= 0
    order = jnp.zeros_like(table)
    for shift in range(1, QB_DEV * TOPK):
        same = (pltpu.roll(owner, shift, 1) == owner) & live
        order = order + same.astype(jnp.int32)
    for k in range(LIVE):
        x = jnp.where(live & (owner == me) & (order == k), inside, 0)
        for shift in (1, 2, 4, 8, 16):
            x = x + pltpu.roll(x, shift, 1)
        plan[k] = x
    plan[LIVE] = jnp.where(live, owner * LIVE + order, -1)
    to_scalar = pltpu.make_async_copy(plan, plan_s, plan_sem)
    to_scalar.start()
    loads[4].wait()
    loads[5].wait()
    to_scalar.wait()
    last = QB_DEV * TOPK - 1

    def pick(d):
        for k in range(LIVE):
            block = plan_s[k, d, last]
            for part in range(BLOCK * heads // 256):
                src = slice(part * 256, (part + 1) * 256)
                dst = slice(part * per, (part + 1) * per)
                split(
                    mem[0, block, src, :],
                    mem[1, block, src, :],
                    put(sent_ref, d, k, 0, dst),
                    put(sent_ref, d, k, 1, dst),
                )

    for k in range(n - 1):
        pick(shifted(k))
        far_copy(0, k).start()
    pick(me)
    near_copy(0).start()

    def send_far(h):
        near_copy(h).start()
        for k in range(n - 1):
            far_copy(h, k).start()

    send_far(1)

    def wait_head(h):
        halo_copy(h).wait_recv()
        near_copy(h).wait()
        for k in range(n - 1):
            far_copy(h, k).wait_recv()

    def finish(h):
        odd = lax.rem(h, 2)

        def piece(t):
            back_copy(h, t).wait_recv()
            rows = pl.ds(pl.multiple_of(t * TILE, TILE), TILE)
            kept = pl.ds(pl.multiple_of(WINDOW + t * TILE, TILE), TILE)
            dkv_ref[h, 0, rows, :] = (
                scale * ka[odd, kept, :] + back[h, t, 0].astype(F32)
            ).astype(BF16)
            dkv_ref[h, 1, rows, :] = (va[odd, kept, :] + back[h, t, 1].astype(F32)).astype(BF16)

        over(0, tiles, piece)

    def head(h):
        wait_head(h)

        @pl.when(h + 2 < heads)
        def _():
            halo_copy(h + 2).start()
            send_far(h + 2)

        odd = lax.rem(h, 2)

        def move(i):
            for s in range(LIVE):
                cur[i * LIVE + s] = recv[h, i, s]

        over(0, n, move)
        kx[:WINDOW, :] = halo[h, 0]
        kx[WINDOW:, :] = own_ref[h, 0]
        vx[:WINDOW, :] = halo[h, 1]
        vx[WINDOW:, :] = own_ref[h, 1]
        ka[odd] = jnp.zeros_like(ka[odd])
        va[odd] = jnp.zeros_like(va[odd])

        def tile(t):
            refs = (
                plan_s, q_ref, g_ref, o_ref, dq_ref, cur,
                kx, vx, km, vm, s_ref, dp_ref, p_ref, ds_ref,
            )
            attend_tile(refs, t, me, h, ka.at[odd], va.at[odd])
            rows = pl.ds(pl.multiple_of(t * TILE, TILE), TILE)
            leave[h, t, 0] = (scale * ka[odd, rows, :]).astype(BF16)
            leave[h, t, 1] = va[odd, rows, :].astype(BF16)
            back_copy(h, t).start()

        over(0, tiles, tile)

        @pl.when(h > 0)
        def _():
            finish(h - 1)

    over(0, heads, head)
    finish(heads - 1)

    over(1, m, lambda r: tab_near(r).wait_send())
    over(1, n, lambda r: tab_far(r).wait_send())

    def drain(h):
        halo_copy(h).wait_send()
        for k in range(n - 1):
            far_copy(h, k).wait_send()
        over(0, tiles, lambda t: back_copy(h, t).wait_send())

    over(0, heads, drain)


def exchange(ids, used, q, g, k, v, mem_k, mem_v, heads, n, m):
    rows = q.shape[0]
    tokens = rows // heads
    tiles = tokens // TILE
    span = WINDOW + TILE
    total = span + TOPK * BLOCK
    halves = TILE // BLOCK
    pairs = heads * tiles * total * TILE
    vmem = pl.BlockSpec(memory_space=pltpu.VMEM)
    smem = pl.BlockSpec(memory_space=pltpu.SMEM)
    hbm = pl.BlockSpec(memory_space=pl.ANY)
    dma = pltpu.SemaphoreType.DMA
    by_head = (heads, tokens, 128)
    by_pair = (heads, 2, tokens, 128)
    return pl.pallas_call(
        functools.partial(exchange_body, heads, n, m),
        in_specs=[smem, smem] + [hbm] * 6,
        out_specs=[vmem, vmem, vmem],
        out_shape=[
            jax.ShapeDtypeStruct(by_head, BF16),
            jax.ShapeDtypeStruct(by_head, BF16),
            jax.ShapeDtypeStruct(by_pair, BF16),
        ],
        scratch_shapes=[
            pltpu.VMEM((4, rows, 128), BF16),
            pltpu.VMEM((2,) + mem_k.shape, BF16),
            pltpu.VMEM(by_head, BF16),
            pltpu.VMEM(by_head, BF16),
            pltpu.VMEM(by_pair, BF16),
            pltpu.VMEM((heads, n, LIVE, 2, BLOCK, 128), BF16),
            pltpu.VMEM((m, 8, 128), jnp.int32),
            pltpu.VMEM((8, 128), jnp.int32),
            pltpu.VMEM((n, 8, 128), jnp.int32),
            pltpu.VMEM((n, 128), jnp.int32),
            pltpu.VMEM((LIVE + 1, n, 128), jnp.int32),
            pltpu.SMEM((LIVE + 1, n, 128), jnp.int32),
            pltpu.VMEM((heads, n, LIVE, 2, BLOCK, 128), BF16),
            pltpu.VMEM((heads, 2, WINDOW, 128), BF16),
            pltpu.VMEM((heads, tiles, 2, TILE, 128), BF16),
            pltpu.VMEM((heads, tiles, 2, TILE, 128), BF16),
            pltpu.VMEM((n * LIVE, 2, BLOCK, 128), BF16),
            pltpu.VMEM((2 * WINDOW, 128), BF16),
            pltpu.VMEM((2 * WINDOW, 128), BF16),
            pltpu.VMEM((halves, TOPK * BLOCK, 128), BF16),
            pltpu.VMEM((halves, TOPK * BLOCK, 128), BF16),
            pltpu.VMEM((total, TILE), F32),
            pltpu.VMEM((total, TILE), F32),
            pltpu.VMEM((total, TILE), BF16),
            pltpu.VMEM((total, TILE), BF16),
            pltpu.VMEM((2, 2 * WINDOW, 128), F32),
            pltpu.VMEM((2, 2 * WINDOW, 128), F32),
            dma((6,)), dma, dma((m,)), dma((m,)), dma((n,)), dma((n,)),
            dma((heads, n)), dma((heads, n)), dma((heads,)),
            dma((heads,)), dma((heads,)), dma((heads, tiles)), dma((heads, tiles)),
        ],
        compiler_params=pltpu.CompilerParams(
            vmem_limit_bytes=VMEM, collective_id=0, has_side_effects=True
        ),
        cost_estimate=pl.CostEstimate(
            flops=pairs * 128 * 12, bytes_accessed=heads * 6 * 2**20, transcendentals=pairs
        ),
        name="exchange_attend",
    )(ids, used, q, g, k, v, mem_k, mem_v)


def join_body(heads, o_ref, dq_ref, dkv_ref, o_out, dq_out, dk_out, dv_out):
    perm = heads_to_rows(256, heads)
    per = 256 // heads
    for part in range(o_out.shape[0] // 256):
        src = slice(part * per, (part + 1) * per)
        dst = slice(part * 256, (part + 1) * 256)
        o = jnp.concatenate([o_ref[h, src, :] for h in range(heads)], 0)
        dq = jnp.concatenate([dq_ref[h, src, :] for h in range(heads)], 0)
        both = dot(perm, jnp.concatenate([o, dq], 1)).astype(BF16)
        o_out[dst, :] = both[:, :128]
        dq_out[dst, :] = both[:, 128:]
        dk = jnp.concatenate([dkv_ref[h, 0, src, :] for h in range(heads)], 0)
        dv = jnp.concatenate([dkv_ref[h, 1, src, :] for h in range(heads)], 0)
        both = dot(perm, jnp.concatenate([dk, dv], 1)).astype(BF16)
        dk_out[dst, :] = both[:, :128]
        dv_out[dst, :] = both[:, 128:]


def join_heads(o, dq, dkv):
    heads, tokens = o.shape[:2]
    steps = 4
    hm = pl.BlockSpec((heads, tokens // steps, 128), lambda i: (0, i, 0))
    kv = pl.BlockSpec((heads, 2, tokens // steps, 128), lambda i: (0, 0, i, 0))
    out = pl.BlockSpec((tokens * heads // steps, 128), lambda i: (i, 0))
    return pl.pallas_call(
        functools.partial(join_body, heads),
        grid=(steps,),
        in_specs=[hm, hm, kv],
        out_specs=[out] * 4,
        out_shape=[jax.ShapeDtypeStruct((tokens * heads, 128), BF16)] * 4,
        compiler_params=pltpu.CompilerParams(vmem_limit_bytes=VMEM),
        cost_estimate=pl.CostEstimate(
            flops=4 * 2 * tokens * heads * 256 * 128,
            bytes_accessed=16 * tokens * heads * 128,
            transcendentals=0,
        ),
        name="join_heads",
    )(o, dq, dkv)


def shards(queries, seg_keys, seg_values, mem_keys, mem_values, mem_blocks, mem_count, grad_out):
    tokens, heads, dim = queries.shape
    mem_local = mem_keys.shape[0] // BLOCK

    def as_rows(x):
        return x.reshape(x.shape[0] * heads, dim)

    def as_blocks(x):
        return x.reshape(mem_local, BLOCK * heads, dim)

    outs = exchange(
        mem_blocks, mem_count,
        as_rows(queries), as_rows(grad_out), as_rows(seg_keys), as_rows(seg_values),
        as_blocks(mem_keys), as_blocks(mem_values),
        heads, lax.axis_size("seq"), lax.axis_size("head"),
    )
    return tuple(x.reshape(tokens, heads, dim) for x in join_heads(*outs))


def solution(mesh):
    wide = P("seq", "head", None)
    return jax.shard_map(
        shards,
        mesh=mesh,
        in_specs=(wide, wide, wide, wide, wide, P(("seq", "head"), None), P(("seq", "head")), wide),
        out_specs=(wide, wide, wide, wide),
        check_vma=False,
    )
```

time: 222 us -> 191 us (0.86)
  Pallas kernels: 214 us -> 189 us
  local copies, waits for them, and re-layouts: 4.09 us -> 0 us
    pallas_call x4 -> x1, Pallas kernels: 209 us -> 184 us  [exchange(): pl.pallas_call(functools.partial(exchange_body, heads, n, m), in_specs=[s...]
where the time goes in v3:
time: 191 us; the launch traced here: 190 us
  Pallas kernels  189 us (99%)
    pallas_call x1, Pallas kernels, exchange(): pl.pallas_call(functools.partial(exchange_body, heads, n, m), in_specs=[s...  184 us
    pallas_call x1, Pallas kernels, join_heads(): pl.pallas_call(functools.partial(join_body, heads), grid=(steps,), in_spe...  5.53 us

profile of v3, /device:TPU:6, one launch (start us, length us, event | category | flops | bytes accessed | tf_op | source)
XLA Modules:
  0.0 190.5 jit_solution(3593287747221267715)
XLA Ops:
  1.3 183.7 %exchange_attend.1 = (bf16[4,1024,128]{2,1,0:T(8,128)(2,1)}, bf16[4,1024,128]{2,1,0:T(8,128)(2,1)}, bf16[4,2,1024,128]{3,2,1,0:T(8,128)(2,1)}) custom-call(s32[1,4]{1,0:T(1,128)} %ids_ref.1, s32[1]{0:T(128)S(6)} %copy.12.used_ref, bf16[4096,128]{1,0:T(8,128)(2,1)} %bitcast.12, bf16[4096,128]{1,0:T(8,128)(2,1)} %bitcast.13, bf16[4096,128]{1,0:T(8,128)(2,1)} %bitcast.14, ...), custom_call_target="tpu_custom_call" | custom-call | flops 11274289152 | bytes 25165824 | tf_op jit(solution)/shard_map/exchange_attend/pallas_call | solution.py:433
  184.9 5.5 %join_heads.1 = (bf16[4096,128]{1,0:T(8,128)(2,1)}, bf16[4096,128]{1,0:T(8,128)(2,1)}, bf16[4096,128]{1,0:T(8,128)(2,1)}, bf16[4096,128]{1,0:T(8,128)(2,1)}) custom-call(bf16[4,1024,128]{2,1,0:T(8,128)(2,1)} %get-tuple-element.11.o_ref, bf16[4,1024,128]{2,1,0:T(8,128)(2,1)} %get-tuple-element.12.dq_ref, bf16[4,2,1024,128]{3,2,1,0:T(8,128)(2,1)} %get-tuple-element.13.dkv_ref), custom_call_target="tpu_custom_call" | custom-call | flops 1073741824 | bytes 8388608 | tf_op jit(solution)/shard_map/join_heads/pallas_call | solution.py:508

commit v4 on v3

--- a/solution.py
+++ b/solution.py
@@ -20,6 +20,7 @@
     (1, 1), (3, 3), (1, 3), (3, 1), (0, 1), (0, 3), (1, 0), (3, 0),
 )
 TILE = 256
+HALF = 512
 VMEM = 60 * 1024 * 1024
 NEG = -1e30
 F32 = jnp.float32
@@ -49,7 +50,7 @@
 
 
 def attend_tile(refs, t, rank, h, ka, va):
-    (plan_s, q_ref, g_ref, o_ref, dq_ref, cur, kx, vx, km, vm, s_ref, dp_ref, p_ref, ds_ref) = refs
+    (plan_s, qg_ref, o_ref, dq_ref, stat, cur, kx, vx, km, vm, s_ref, dp_ref, p_ref, ds_ref) = refs
     span = WINDOW + TILE
     total = span + TOPK * BLOCK
     halves = TILE // BLOCK
@@ -57,8 +58,8 @@
     to_two = scale * math.log2(math.e)
     start = pl.multiple_of(t * TILE, TILE)
     win = pl.ds(start, span)
-    q = q_ref[h, pl.ds(start, TILE), :]
-    g = g_ref[h, pl.ds(start, TILE), :]
+    q = qg_ref[h, 0, pl.ds(start, TILE), :]
+    g = qg_ref[h, 1, pl.ds(start, TILE), :]
 
     for half in range(halves):
         for e in range(TOPK):
@@ -103,31 +104,29 @@
     def top_step(c, top):
         return jnp.maximum(top, fold(s_ref[chunk(c), :], jnp.max))
 
-    top = lax.fori_loop(0, steps, top_step, jnp.full((8, TILE), NEG, F32), unroll=2)
+    top = lax.fori_loop(0, steps, top_step, jnp.full((8, TILE), NEG, F32), unroll=7)
     top = jnp.max(top, 0, keepdims=True) * to_two
 
-    def exp_step(c, acc):
+    def exp_step(c, accs):
         e = jnp.exp2(s_ref[chunk(c), :] * to_two - top)
         s_ref[chunk(c), :] = e
-        return acc + fold(e, jnp.sum)
-
-    acc = lax.fori_loop(0, steps, exp_step, jnp.zeros((8, TILE), F32), unroll=2)
-    inv = 1.0 / jnp.sum(acc, 0, keepdims=True)
-
-    def prob_step(c, acc):
+        return accs[0] + fold(e, jnp.sum), accs[1] + fold(e * dp_ref[chunk(c), :], jnp.sum)
+
+    zero = jnp.zeros((8, TILE), F32)
+    mass, delta = lax.fori_loop(0, steps, exp_step, (zero, zero), unroll=7)
+    mass = jnp.sum(mass, 0, keepdims=True)
+    inv = 1.0 / mass
+    delta = jnp.sum(delta, 0, keepdims=True) * inv
+    stat[h, t, 0:1, :] = top + jnp.log(mass) * math.log2(math.e)
+    stat[h, t, 1:2, :] = delta
+
+    def prob_step(c, carry):
         p = s_ref[chunk(c), :] * inv
-        s_ref[chunk(c), :] = p
         p_ref[chunk(c), :] = p.astype(BF16)
-        return acc + fold(p * dp_ref[chunk(c), :], jnp.sum)
-
-    acc = lax.fori_loop(0, steps, prob_step, jnp.zeros((8, TILE), F32), unroll=2)
-    delta = jnp.sum(acc, 0, keepdims=True)
-
-    def score_step(c, carry):
-        ds_ref[chunk(c), :] = (s_ref[chunk(c), :] * (dp_ref[chunk(c), :] - delta)).astype(BF16)
+        ds_ref[chunk(c), :] = (p * (dp_ref[chunk(c), :] - delta)).astype(BF16)
         return carry
 
-    lax.fori_loop(0, steps, score_step, 0, unroll=2)
+    lax.fori_loop(0, steps, prob_step, 0, unroll=7)
 
     o = dot(p_ref[:span, :], vx[win, :], TN)
     dq = dot(ds_ref[:span, :], kx[win, :], TN)
@@ -138,17 +137,48 @@
         dq_ref[h, dst, :] = (
             scale * (dq[cols] + dot(ds_ref[span:, cols], km[half], TN))
         ).astype(BF16)
-    va[win, :] += dot(p_ref[:span, :], g)
-    ka[win, :] += dot(ds_ref[:span, :], q)
+
+    def own_keys(b, carry):
+        src = pl.ds(pl.multiple_of(WINDOW + (b - t) * TILE, TILE), TILE)
+        dst = pl.ds(pl.multiple_of(b * TILE, TILE), TILE)
+        va[dst, :] += dot(p_ref[src, :], g)
+        ka[dst, :] += dot(ds_ref[src, :], q)
+        return carry
+
+    lax.fori_loop(0, t + 1, own_keys, 0)
+
+
+def next_tile(h, t, rank, n, own_ref, next_ref, stat_in, ka, va):
+    scale = 1.0 / math.sqrt(128.0)
+    to_two = scale * math.log2(math.e)
+    cols = pl.ds(pl.multiple_of(t * TILE, TILE), TILE)
+    q = next_ref[h, 0, cols, :]
+    g = next_ref[h, 1, cols, :]
+    lse = jnp.where(rank == n - 1, -NEG, stat_in[h, t, 0:1, :])
+    delta = stat_in[h, t, 1:2, :]
+    row = lax.broadcasted_iota(jnp.int32, (TILE, TILE), 0)
+    col = lax.broadcasted_iota(jnp.int32, (TILE, TILE), 1)
+
+    def keys(b, carry):
+        rows = pl.ds(pl.multiple_of(b * TILE, TILE), TILE)
+        s = dot(own_ref[h, 0, rows, :], q, NT)
+        s = jnp.where(row + (b - t) * TILE > col, s * to_two, NEG)
+        p = jnp.exp2(s - lse)
+        ds = p * (dot(own_ref[h, 1, rows, :], g, NT) - delta)
+        va[rows, :] += dot(p.astype(BF16), g)
+        ka[rows, :] += dot(ds.astype(BF16), q)
+        return carry
+
+    lax.fori_loop(t, WINDOW // TILE, keys, 0)
 
 
 def exchange_body(
     heads, n, m, ids_ref, used_ref, q_hbm, g_hbm, k_hbm, v_hbm, mk_hbm, mv_hbm,
     o_ref, dq_ref, dkv_ref,
-    raw, mem, q_ref, g_ref, own_ref, sent_ref, near_tab, my_tab, far_tab, flat, plan, plan_s,
-    recv, halo, leave, back, cur, kx, vx, km, vm, s_ref, dp_ref, p_ref, ds_ref, ka, va,
+    raw, mem, qg_ref, own_ref, sent_ref, near_tab, my_tab, far_tab, flat, plan, plan_s,
+    recv, halo, ahead, stat, stat_in, cur, kx, vx, km, vm, s_ref, dp_ref, p_ref, ds_ref, ka, va,
     load_sem, plan_sem, tab_near_send, tab_near_recv, tab_far_send, tab_far_recv,
-    far_send, far_recv, near, halo_send, halo_recv, back_send, back_recv,
+    far_send, far_recv, near, halo_send, halo_recv, ahead_send, ahead_recv, stat_send, stat_recv,
 ):
     me = lax.axis_index("seq")
     hd = lax.axis_index("head")
@@ -224,23 +254,40 @@
     def near_copy(h):
         return pltpu.make_async_copy(sent_ref.at[h, me], recv.at[h, me], near.at[h])
 
-    def halo_copy(h):
+    def quarter(j):
+        return pl.ds((j % 2) * HALF, HALF)
+
+    def halo_copy(h, j):
         return pltpu.make_async_remote_copy(
-            src_ref=own_ref.at[h],
-            dst_ref=halo.at[h],
-            send_sem=halo_send.at[h],
-            recv_sem=halo_recv.at[h],
+            src_ref=own_ref.at[h, j // 2, quarter(j)],
+            dst_ref=halo.at[h, j // 2, quarter(j)],
+            send_sem=halo_send.at[h, j],
+            recv_sem=halo_recv.at[h, j],
             device_id={"seq": peer(1)},
         )
 
-    def back_copy(h, t):
+    def ahead_copy(h, j):
         return pltpu.make_async_remote_copy(
-            src_ref=leave.at[h, t],
-            dst_ref=back.at[h, t],
-            send_sem=back_send.at[h, t],
-            recv_sem=back_recv.at[h, t],
+            src_ref=qg_ref.at[h, j // 2, quarter(j)],
+            dst_ref=ahead.at[h, j // 2, quarter(j)],
+            send_sem=ahead_send.at[h, j],
+            recv_sem=ahead_recv.at[h, j],
             device_id={"seq": peer(n - 1)},
         )
+
+    def stat_copy(h):
+        return pltpu.make_async_remote_copy(
+            src_ref=stat.at[h],
+            dst_ref=stat_in.at[h],
+            send_sem=stat_send.at[h],
+            recv_sem=stat_recv.at[h],
+            device_id={"seq": peer(n - 1)},
+        )
+
+    def each_part(what):
+        for h in range(heads):
+            for j in range(4):
+                what(h, j)
 
     over(1, m, lambda r: tab_near(r).start())
 
@@ -271,14 +318,14 @@
 
     def split_qg(i):
         src, dst = spans(i)
-        split(raw[2, src, :], raw[3, src, :], put(q_ref, dst), put(g_ref, dst))
+        split(raw[2, src, :], raw[3, src, :], put(qg_ref, 0, dst), put(qg_ref, 1, dst))
 
     parts = WINDOW * heads // 256
     loads[0].wait()
     loads[1].wait()
     over(0, parts, split_kv, unroll=2)
-    halo_copy(0).start()
-    halo_copy(1).start()
+    for j in range(4):
+        halo_copy(0, j).start()
 
     over(1, m, lambda r: tab_near(r).wait_recv())
     total = near_tab[0]
@@ -291,6 +338,8 @@
     loads[2].wait()
     loads[3].wait()
     over(0, parts, split_qg, unroll=2)
+    for j in range(4):
+        ahead_copy(0, j).start()
     over(1, n, lambda r: tab_far(r).wait_recv())
 
     for d in range(n):
@@ -329,46 +378,42 @@
                     put(sent_ref, d, k, 1, dst),
                 )
 
+    def follow(h, k):
+        @pl.when(h < heads)
+        def _():
+            if k == 0:
+                near_copy(h).start()
+            if k % 4 == 0:
+                halo_copy(h, k // 4).start()
+                ahead_copy(h, k // 4).start()
+            far_copy(h, k).start()
+
     for k in range(n - 1):
         pick(shifted(k))
         far_copy(0, k).start()
     pick(me)
     near_copy(0).start()
 
-    def send_far(h):
-        near_copy(h).start()
-        for k in range(n - 1):
-            far_copy(h, k).start()
-
-    send_far(1)
-
-    def wait_head(h):
-        halo_copy(h).wait_recv()
+    def finish(h):
+        odd = lax.rem(h, 2)
+        stat_copy(h).wait_recv()
+        for j in range(4):
+            ahead_copy(h, j).wait_recv()
+        over(
+            0,
+            tiles,
+            lambda t: next_tile(h, t, me, n, own_ref, ahead, stat_in, ka.at[odd], va.at[odd]),
+        )
+        dkv_ref[h, 0] = (scale * ka[odd]).astype(BF16)
+        dkv_ref[h, 1] = va[odd].astype(BF16)
+
+    def head(h):
         near_copy(h).wait()
+        for j in range(4):
+            halo_copy(h, j).wait_recv()
         for k in range(n - 1):
             far_copy(h, k).wait_recv()
-
-    def finish(h):
-        odd = lax.rem(h, 2)
-
-        def piece(t):
-            back_copy(h, t).wait_recv()
-            rows = pl.ds(pl.multiple_of(t * TILE, TILE), TILE)
-            kept = pl.ds(pl.multiple_of(WINDOW + t * TILE, TILE), TILE)
-            dkv_ref[h, 0, rows, :] = (
-                scale * ka[odd, kept, :] + back[h, t, 0].astype(F32)
-            ).astype(BF16)
-            dkv_ref[h, 1, rows, :] = (va[odd, kept, :] + back[h, t, 1].astype(F32)).astype(BF16)
-
-        over(0, tiles, piece)
-
-    def head(h):
-        wait_head(h)
-
-        @pl.when(h + 2 < heads)
-        def _():
-            halo_copy(h + 2).start()
-            send_far(h + 2)
+            follow(h + 1, k)
 
         odd = lax.rem(h, 2)
 
@@ -386,16 +431,13 @@
 
         def tile(t):
             refs = (
-                plan_s, q_ref, g_ref, o_ref, dq_ref, cur,
+                plan_s, qg_ref, o_ref, dq_ref, stat, cur,
                 kx, vx, km, vm, s_ref, dp_ref, p_ref, ds_ref,
             )
             attend_tile(refs, t, me, h, ka.at[odd], va.at[odd])
-            rows = pl.ds(pl.multiple_of(t * TILE, TILE), TILE)
-            leave[h, t, 0] = (scale * ka[odd, rows, :]).astype(BF16)
-            leave[h, t, 1] = va[odd, rows, :].astype(BF16)
-            back_copy(h, t).start()
 
         over(0, tiles, tile)
+        stat_copy(h).start()
 
         @pl.when(h > 0)
         def _():
@@ -407,11 +449,13 @@
     over(1, m, lambda r: tab_near(r).wait_send())
     over(1, n, lambda r: tab_far(r).wait_send())
 
+    each_part(lambda h, j: halo_copy(h, j).wait_send())
+    each_part(lambda h, j: ahead_copy(h, j).wait_send())
+
     def drain(h):
-        halo_copy(h).wait_send()
+        stat_copy(h).wait_send()
         for k in range(n - 1):
             far_copy(h, k).wait_send()
-        over(0, tiles, lambda t: back_copy(h, t).wait_send())
 
     over(0, heads, drain)
 
@@ -442,8 +486,7 @@
         scratch_shapes=[
             pltpu.VMEM((4, rows, 128), BF16),
             pltpu.VMEM((2,) + mem_k.shape, BF16),
-            pltpu.VMEM(by_head, BF16),
-            pltpu.VMEM(by_head, BF16),
+            pltpu.VMEM(by_pair, BF16),
             pltpu.VMEM(by_pair, BF16),
             pltpu.VMEM((heads, n, LIVE, 2, BLOCK, 128), BF16),
             pltpu.VMEM((m, 8, 128), jnp.int32),
@@ -453,9 +496,10 @@
             pltpu.VMEM((LIVE + 1, n, 128), jnp.int32),
             pltpu.SMEM((LIVE + 1, n, 128), jnp.int32),
             pltpu.VMEM((heads, n, LIVE, 2, BLOCK, 128), BF16),
-            pltpu.VMEM((heads, 2, WINDOW, 128), BF16),
-            pltpu.VMEM((heads, tiles, 2, TILE, 128), BF16),
-            pltpu.VMEM((heads, tiles, 2, TILE, 128), BF16),
+            pltpu.VMEM(by_pair, BF16),
+            pltpu.VMEM(by_pair, BF16),
+            pltpu.VMEM((heads, tiles, 8, TILE), F32),
+            pltpu.VMEM((heads, tiles, 8, TILE), F32),
             pltpu.VMEM((n * LIVE, 2, BLOCK, 128), BF16),
             pltpu.VMEM((2 * WINDOW, 128), BF16),
             pltpu.VMEM((2 * WINDOW, 128), BF16),
@@ -465,11 +509,12 @@
             pltpu.VMEM((total, TILE), F32),
             pltpu.VMEM((total, TILE), BF16),
             pltpu.VMEM((total, TILE), BF16),
-            pltpu.VMEM((2, 2 * WINDOW, 128), F32),
-            pltpu.VMEM((2, 2 * WINDOW, 128), F32),
+            pltpu.VMEM((2, WINDOW, 128), F32),
+            pltpu.VMEM((2, WINDOW, 128), F32),
             dma((6,)), dma, dma((m,)), dma((m,)), dma((n,)), dma((n,)),
             dma((heads, n)), dma((heads, n)), dma((heads,)),
-            dma((heads,)), dma((heads,)), dma((heads, tiles)), dma((heads, tiles)),
+            dma((heads, 4)), dma((heads, 4)), dma((heads, 4)), dma((heads, 4)),
+            dma((heads,)), dma((heads,)),
         ],
         compiler_params=pltpu.CompilerParams(
             vmem_limit_bytes=VMEM, collective_id=0, has_side_effects=True

time: 191 us -> 190 us (level)
  Pallas kernels: 189 us -> 187 us
    pallas_call x1, Pallas kernels: 184 us -> 181 us  [exchange(): pl.pallas_call(functools.partial(exchange_body, heads, n, m), in_specs=[s...]
where the time goes in v4:
time: 190 us; the launch traced here: 188 us
  Pallas kernels  187 us (98%)
    pallas_call x1, Pallas kernels, exchange(): pl.pallas_call(functools.partial(exchange_body, heads, n, m), in_specs=[s...  181 us
    pallas_call x1, Pallas kernels, join_heads(): pl.pallas_call(functools.partial(join_body, heads), grid=(steps,), in_spe...  5.52 us

profile of v4, /device:TPU:6, one launch (start us, length us, event | category | flops | bytes accessed | tf_op | source)
XLA Modules:
  0.0 188.0 jit_solution(17174688455944138728)
XLA Ops:
  1.3 181.2 %exchange_attend.1 = (bf16[4,1024,128]{2,1,0:T(8,128)(2,1)}, bf16[4,1024,128]{2,1,0:T(8,128)(2,1)}, bf16[4,2,1024,128]{3,2,1,0:T(8,128)(2,1)}) custom-call(s32[1,4]{1,0:T(1,128)} %ids_ref.1, s32[1]{0:T(128)S(6)} %copy.12.used_ref, bf16[4096,128]{1,0:T(8,128)(2,1)} %bitcast.12, bf16[4096,128]{1,0:T(8,128)(2,1)} %bitcast.13, bf16[4096,128]{1,0:T(8,128)(2,1)} %bitcast.14, ...), custom_call_target="tpu_custom_call" | custom-call | flops 11274289152 | bytes 25165824 | tf_op jit(solution)/shard_map/exchange_attend/pallas_call | solution.py:477
  182.5 5.5 %join_heads.1 = (bf16[4096,128]{1,0:T(8,128)(2,1)}, bf16[4096,128]{1,0:T(8,128)(2,1)}, bf16[4096,128]{1,0:T(8,128)(2,1)}, bf16[4096,128]{1,0:T(8,128)(2,1)}) custom-call(bf16[4,1024,128]{2,1,0:T(8,128)(2,1)} %get-tuple-element.11.o_ref, bf16[4,1024,128]{2,1,0:T(8,128)(2,1)} %get-tuple-element.12.dq_ref, bf16[4,2,1024,128]{3,2,1,0:T(8,128)(2,1)} %get-tuple-element.13.dkv_ref), custom_call_target="tpu_custom_call" | custom-call | flops 1073741824 | bytes 8388608 | tf_op jit(solution)/shard_map/join_heads/pallas_call | solution.py:553
